TPU v7x, 256 devices: a whole 4x4x8 slice. The times are simulated.
256 devices in a mesh: ctx: 32 (over z, x), rep: 8 (over y, core).
Axes of the slice: x: 4, y: 4, z: 8, core: 2. Of those that a mesh axis runs over, the one named last changes fastest.
Arguments:
- query: bfloat16 [32768, 2048], P(('rep', 'ctx')), parts along dimension 0, may hold values from -6 to 6
- key: bfloat16 [32768, 2048], P(('rep', 'ctx')), parts along dimension 0, may hold values from -6 to 6
- value: bfloat16 [32768, 2048], P(('rep', 'ctx')), parts along dimension 0, may hold values from -6 to 6
- beta: float32 [32768, 16], P(('rep', 'ctx')), parts along dimension 0, may hold values from 0.05 to 0.95
- log_gate: float32 [32768, 16], P(('rep', 'ctx')), parts along dimension 0, may hold values from -1.5 to 0
- level_weight: float32 [32768, 16, 6], P(('rep', 'ctx')), parts along dimension 0, may hold values from 0.1 to 1.5
- norm_gain: float32 [128], replicated, may hold values from 0.5 to 1.5
- grad_out: bfloat16 [32768, 2048], P(('rep', 'ctx')), parts along dimension 0, may hold values from -6 to 6
- grad_final_state: float32 [16384, 128], P(('rep', 'ctx')), parts along dimension 0, may hold values from -6 to 6
Outputs:
- grad_query: bfloat16 [32768, 2048], P(('rep', 'ctx')), parts along dimension 0
- grad_key: bfloat16 [32768, 2048], P(('rep', 'ctx')), parts along dimension 0
- grad_value: bfloat16 [32768, 2048], P(('rep', 'ctx')), parts along dimension 0
- grad_beta: float32 [32768, 16], P(('rep', 'ctx')), parts along dimension 0
- grad_level: float32 [32768, 16, 6], P(('rep', 'ctx')), parts along dimension 0
- grad_gain: float32 [1024], P('rep'), parts along dimension 0
- final_state: float32 [16384, 128], P(('rep', 'ctx')), parts along dimension 0
There are 8 independent parts, one for each index of `rep`. A program takes and returns all parts, laid end to end along the dimension named above; an argument that names none is the same for every part. Nothing has to cross between parts.
All inputs are finite; a program needn't handle non-finite values.
Results may differ from a plain program's by a relative error of at most 0.001.
Values sent between devices are 32-bit elements; how exact they have to be, the bound alone decides.
No kernel may reach another device: no remote copies, remote signals or barrier semaphores. Data moves between devices by JAX's collectives and lax.ppermute only.
A program may use at most 128 MiB of HBM per device.

v0:
```python
import jax
import jax.numpy as jnp
from jax import lax
from jax.sharding import PartitionSpec as P

epsilon = 1e-06
topmost_level = lax.Precision.HIGHEST


def from_partner(value, axis, bit):
    mask = 2**bit
    pairs = [(source, source ^ mask) for source in range(lax.axis_size(axis))]
    return lax.ppermute(value, axis, pairs)


def normalize(values):
    return values * lax.rsqrt(jnp.sum(values * values, axis=-1, keepdims=True) + epsilon)


def split_heads(values, head_count):
    row_count = values.shape[0]
    return values.reshape(row_count, head_count, -1).transpose(1, 0, 2)


def prepare(query, key, value, beta, cum_gate):
    head_count = cum_gate.shape[0]
    row_count = cum_gate.shape[1]
    query_normed = normalize(split_heads(query, head_count))
    normalized_key = normalize(split_heads(key, head_count))
    value_heads = split_heads(value, head_count)
    beta_heads = beta.T
    strict = jnp.tril(jnp.ones((row_count, row_count), dtype=bool), -1)
    log_gaps = cum_gate[:, :, None] - cum_gate[:, None, :]
    decays = jnp.exp(jnp.where(strict[None], log_gaps, -jnp.inf))
    key_inner = jnp.einsum("htk,hsk->hts", normalized_key, normalized_key, precision=topmost_level)
    system = (
        jnp.eye(row_count, dtype=cum_gate.dtype)[None] + beta_heads[:, :, None] * decays * key_inner
    )
    surrogate_value = jax.scipy.linalg.solve_triangular(
        system, beta_heads[:, :, None] * value_heads, lower=True
    )
    trailing_decay = jnp.exp(cum_gate[:, -1:] - cum_gate)
    state_per_block = jnp.einsum(
        "fni,fnb->fib",
        normalized_key * trailing_decay[:, :, None],
        surrogate_value,
        precision=topmost_level,
    )
    return (query_normed, normalized_key, surrogate_value, state_per_block)


def finish(
    query_normed, normalized_key, surrogate_value, level_weight, norm_gain, bucket_states, cum_gate
):
    row_count = cum_gate.shape[1]
    inclusive = jnp.tril(jnp.ones((row_count, row_count), dtype=bool))
    log_gaps = cum_gate[:, :, None] - cum_gate[:, None, :]
    decays = jnp.exp(jnp.where(inclusive[None], log_gaps, -jnp.inf))
    attention_scores = (
        jnp.einsum("htk,hsk->hts", query_normed, normalized_key, precision=topmost_level) * decays
    )
    intra_out = jnp.einsum(
        "hts,hsv->htv", attention_scores, surrogate_value, precision=topmost_level
    )
    cross_out = jnp.einsum("htk,lhkv->lhtv", query_normed, bucket_states, precision=topmost_level)
    level_heads = level_weight.transpose(1, 0, 2)
    weighted = level_heads[:, :, 1:] * jnp.exp(cum_gate)[:, :, None]
    mixture = level_heads[:, :, 0:1] * intra_out + jnp.einsum(
        "htl,lhtv->htv", weighted, cross_out, precision=topmost_level
    )
    inverse_rms = lax.rsqrt(jnp.mean(mixture * mixture, axis=-1, keepdims=True) + epsilon)
    normed = mixture * inverse_rms * norm_gain
    return normed.transpose(1, 0, 2).reshape(row_count, -1)


def local(query, key, value, beta, log_gate, level_weight, norm_gain, grad_out, grad_final_state):
    levels = level_weight.shape[2]
    cum_gate = jnp.cumsum(log_gate.T, axis=1)
    block_grand_total = cum_gate[:, -1]

    def local_prepare(query_float, key_float, value_float, beta_float):
        return prepare(query_float, key_float, value_float, beta_float, cum_gate)

    prepared, prepare_back = jax.vjp(
        local_prepare,
        query.astype(jnp.float32),
        key.astype(jnp.float32),
        value.astype(jnp.float32),
        beta,
    )
    query_normed, normalized_key, surrogate_value, state_per_block = prepared
    device = lax.axis_index("ctx")
    aggregate = state_per_block
    group_total = block_grand_total
    offset = jnp.zeros_like(block_grand_total)
    records = []
    bucket_list = []
    for degree in range(levels - 1):
        is_upper = device >> degree & 1 == 1
        if degree < levels - 2:
            partner, partner_total = from_partner((aggregate, group_total), "ctx", degree)
        else:
            partner, partner_total = from_partner((aggregate, group_total), "ctx", degree)
        bucket_list.append(jnp.where(is_upper, jnp.exp(offset)[:, None, None] * partner, 0.0))
        records.append((is_upper, offset, group_total, partner_total))
        aggregate = jnp.where(
            is_upper,
            jnp.exp(group_total)[:, None, None] * partner + aggregate,
            jnp.exp(partner_total)[:, None, None] * aggregate + partner,
        )
        offset = jnp.where(is_upper, offset + partner_total, offset)
        group_total = group_total + partner_total
    bucket_stack = jnp.stack(bucket_list)
    rows_dev = grad_final_state.shape[0]
    rows_total = aggregate.shape[0] * aggregate.shape[1]
    full_rows = aggregate.reshape(rows_total, -1)
    own_rows = lax.dynamic_slice_in_dim(full_rows, device * rows_dev, rows_dev, 0)

    def local_finish(normed_queries, normed_keys, pseudo_rows, level_rows, gain_rows, bucket_rows):
        return finish(
            normed_queries, normed_keys, pseudo_rows, level_rows, gain_rows, bucket_rows, cum_gate
        )

    mixed_out, finish_back = jax.vjp(
        local_finish,
        query_normed,
        normalized_key,
        surrogate_value,
        level_weight,
        norm_gain,
        bucket_stack,
    )
    grad_qnormed, grad_knormed, grad_pseudo, grad_level, grad_gain_local, grad_buckets = (
        finish_back(grad_out.astype(jnp.float32))
    )
    seed_rows = lax.dynamic_update_slice_in_dim(
        jnp.zeros((rows_total, grad_final_state.shape[1]), jnp.float32),
        grad_final_state,
        device * rows_dev,
        0,
    )
    adjoint = seed_rows.reshape(state_per_block.shape)
    for degree in reversed(range(levels - 1)):
        is_upper, offset, group_total, partner_total = records[degree]
        outgoing = jnp.where(
            is_upper,
            jnp.exp(offset)[:, None, None] * grad_buckets[degree]
            + jnp.exp(group_total)[:, None, None] * adjoint,
            adjoint,
        )
        retained = jnp.where(is_upper, adjoint, jnp.exp(partner_total)[:, None, None] * adjoint)
        incoming = from_partner(outgoing, "ctx", degree)
        adjoint = retained + incoming
    grad_query, grad_key, grad_value, grad_beta = prepare_back(
        (grad_qnormed, grad_knormed, grad_pseudo, adjoint)
    )
    grad_gain = lax.psum(grad_gain_local, "ctx")
    return (
        grad_query.astype(jnp.bfloat16),
        grad_key.astype(jnp.bfloat16),
        grad_value.astype(jnp.bfloat16),
        grad_beta,
        grad_level,
        grad_gain,
        own_rows,
    )


def solution(mesh):
    in_specs = (
        P(("rep", "ctx"), None),
        P(("rep", "ctx"), None),
        P(("rep", "ctx"), None),
        P(("rep", "ctx"), None),
        P(("rep", "ctx"), None),
        P(("rep", "ctx"), None, None),
        P(),
        P(("rep", "ctx"), None),
        P(("rep", "ctx"), None),
    )
    out_specs = (
        P(("rep", "ctx"), None),
        P(("rep", "ctx"), None),
        P(("rep", "ctx"), None),
        P(("rep", "ctx"), None),
        P(("rep", "ctx"), None, None),
        P("rep"),
        P(("rep", "ctx"), None),
    )
    return jax.shard_map(local, mesh=mesh, in_specs=in_specs, out_specs=out_specs, check_vma=False)
```

profile of v0, /device:TPU:16, one launch (start us, length us, event | category | flops | bytes accessed | tf_op | source)
XLA Modules:
  0.0 612.7 jit_solution(5073137040125510307)
XLA Ops:
  0.7 1.3 copy.56
  2.2 1.6 copy.49
  4.5 1.9 fusion.80
  6.4 1.0 copy-done.12
  7.4 0.7 fusion.26
  8.1 157.8 %custom-call.7 = f32[16,1,128,128]{2,3,1,0:T(8,128)} custom-call(f32[16,1,128,128]{3,2,1,0:T(8,128)S(1)} %fusion.26), custom_call_target="InvertDiagBlocksLowerTriangular" | custom-call | tf_op jit(solution)/shard_map/jvp(jit(_solve_triangular))/vmap()/triangular_solve | solution.py:39
  166.0 3.4 fusion.53
  169.4 2.2 fusion.63
  171.6 1.5 collective-permute-start
  173.6 23.2 %collective-permute-done.1 = f32[16]{0:T(128)S(1)} collective-permute-done((f32[16]{0:T(128)S(1)}, f32[16]{0:T(128)S(1)}, u32[]{:S(2)}, u32[]{:S(2)}) %collective-permute-start.1) | collective-permute-done | bytes 96 | tf_op jit(solution)/shard_map/ppermute | solution.py:13
  196.8 3.0 collective-permute-start.3
  199.9 2.0 collective-permute-done.3
  201.9 1.9 collective-permute-start.5
  203.8 1.7 collective-permute-done.5
  205.5 3.3 collective-permute-start.7
  208.8 1.5 collective-permute-done.7
  210.4 1.8 add_select_fusion.4
  212.2 3.4 collective-permute-start.2
  215.6 19.5 %collective-permute-done.2 = f32[16,128,128]{2,1,0:T(8,128)S(1)} collective-permute-done((f32[16,128,128]{2,1,0:T(8,128)S(1)}, f32[16,128,128]{2,1,0:T(8,128)S(1)}, u32[]{:S(2)}, u32[]{:S(2)}) %collective-permute-start.2) | collective-permute-done | bytes 1048608 | tf_op jit(solution)/shard_map/ppermute | solution.py:13
  235.1 1.4 add_select_fusion.3
  236.5 1.7 collective-permute-start.4
  238.2 1.2 copy.48
  239.5 2.2 copy.47
  241.9 16.2 %collective-permute-done.4 = f32[16,128,128]{2,1,0:T(8,128)} collective-permute-done((f32[16,128,128]{2,1,0:T(8,128)}, f32[16,128,128]{2,1,0:T(8,128)}, u32[]{:S(2)}, u32[]{:S(2)}) %collective-permute-start.4) | collective-permute-done | bytes 1048608 | tf_op jit(solution)/shard_map/ppermute | solution.py:13
  258.1 1.8 add_select_fusion.2
  259.9 2.6 collective-permute-start.6
  262.6 2.0 convolution_multiply_fusion.1
  264.7 37.0 %collective-permute-done.6 = f32[16,128,128]{2,1,0:T(8,128)S(1)} collective-permute-done((f32[16,128,128]{2,1,0:T(8,128)S(1)}, f32[16,128,128]{2,1,0:T(8,128)S(1)}, u32[]{:S(2)}, u32[]{:S(2)}) %collective-permute-start.6) | collective-permute-done | bytes 1048608 | tf_op jit(solution)/shard_map/ppermute | solution.py:13
  301.9 6.1 collective-permute-start.8
  308.2 1.4 bitcast_dynamic-update-slice_fusion.2
  309.7 42.9 %collective-permute-done.8 = f32[16,128,128]{2,1,0:T(8,128)S(1)} collective-permute-done((f32[16,128,128]{2,1,0:T(8,128)S(1)}, f32[16,128,128]{2,1,0:T(8,128)S(1)}, u32[]{:S(2)}, u32[]{:S(2)}) %collective-permute-start.8) | collective-permute-done | bytes 1048608 | tf_op jit(solution)/shard_map/ppermute | solution.py:13
  352.8 8.4 %fusion.1 = (f32[16,128,128]{1,2,0:T(8,128)S(1)}, f32[16,5,128,128]{3,2,1,0:T(8,128)S(1)}) fusion(f32[16,128,5]{1,2,0:T(8,128)S(1)} %copy.121, f32[16,128,128]{1,2,0:T(8,128)S(1)} %bitcast.208, f32[16,128]{1,0:T(8,128)S(1)} %add_rsqrt_fusion.1, f32[5,16,128,128]{3,2,1,0:T(8,128)S(1)} %bitcast_dynamic-update-slice_fusion), kind=kOutput, calls=%fused_computation.3 | convolution fusion | flops 2015887360 | bytes 12632064 | tf_op jit(solution)/shard_map/jvp(htk,lhkv->lhtv)/dot_general | solution.py:65
  361.3 1.9 multiply_reduce_fusion.5
  363.9 1.8 fusion
  365.7 6.1 fusion.8
  372.1 3.5 collective-permute-start.10
  375.6 2.5 collective-permute-start.9
  378.1 35.8 %collective-permute-done.9 = f32[16]{0:T(128)S(1)} collective-permute-done((f32[16]{0:T(128)S(1)}, f32[16]{0:T(128)S(1)}, u32[]{:S(2)}, u32[]{:S(2)}) %collective-permute-start.9) | collective-permute-done | bytes 96 | tf_op jit(solution)/shard_map/ppermute | solution.py:13
  414.5 35.2 %collective-permute-done.11 = f32[16,128,128]{2,1,0:T(8,128)S(1)} collective-permute-done((f32[16,128,128]{2,1,0:T(8,128)S(1)}, f32[16,128,128]{2,1,0:T(8,128)S(1)}, u32[]{:S(2)}, u32[]{:S(2)}) %collective-permute-start.11) | collective-permute-done | bytes 1048608 | tf_op jit(solution)/shard_map/ppermute | solution.py:13
  449.7 1.5 fusion.42
  451.3 6.0 collective-permute-start.12
  457.3 2.1 convolution_multiply_fusion
  459.4 21.3 %collective-permute-done.12 = f32[16,128,128]{2,1,0:T(8,128)S(1)} collective-permute-done((f32[16,128,128]{2,1,0:T(8,128)S(1)}, f32[16,128,128]{2,1,0:T(8,128)S(1)}, u32[]{:S(2)}, u32[]{:S(2)}) %collective-permute-start.12) | collective-permute-done | bytes 1048608 | tf_op jit(solution)/shard_map/ppermute | solution.py:13
  480.6 1.4 fusion.39
  482.0 3.0 collective-permute-start.13
  485.1 2.3 fusion.77
  487.4 6.1 multiply_reduce_fusion.3
  493.4 1.0 fusion.28
  494.5 2.0 copy.79
  496.5 79.0 %psum.7 = f32[128]{0:T(128)} all-reduce(f32[128]{0:T(128)S(1)} %get-tuple-element.22), channel_id=1, replica_groups=mesh['ctx'=32,'rep'=8] {'ctx'}, use_global_device_ids=true, to_apply=%region_11.13 | all-reduce | flops 128 | bytes 1024 | tf_op jit(solution)/shard_map/psum | solution.py:157
  575.5 2.8 fusion.36
  579.5 1.9 fusion.59
  581.4 1.1 fusion.66
  582.6 1.4 constant_dynamic-slice_fusion
  583.9 9.7 %collective-permute-done.14 = f32[16,128,128]{2,1,0:T(8,128)S(1)} collective-permute-done((f32[16,128,128]{2,1,0:T(8,128)S(1)}, f32[16,128,128]{2,1,0:T(8,128)S(1)}, u32[]{:S(2)}, u32[]{:S(2)}) %collective-permute-start.14) | collective-permute-done | bytes 1048608 | tf_op jit(solution)/shard_map/ppermute | solution.py:13
  593.6 2.0 convolution_add_fusion
  595.6 2.3 fusion.131
  598.0 1.6 fusion.54
  599.6 2.5 fusion.27
  602.1 1.5 fusion.72
  603.6 2.6 fusion.111
  606.2 2.7 multiply_reduce_fusion.2
  609.6 1.0 copy.80
  610.9 1.0 copy.81
  (89 shorter events, 6.8 us)
Async XLA Ops:
  0.6 3.4 copy-start.20
  0.6 6.8 %copy-start.17 = (f32[128,16]{0,1:T(8,128)S(1)}, f32[128,16]{0,1:T(8,128)}, u32[]{:S(2)}) copy-start(f32[128,16]{0,1:T(8,128)} %param.14) | copy-start | bytes 24580
  2.2 169.4 %copy-start.8 = (f32[128,16,128]{2,0,1:T(8,128)}, f32[128,16,128]{2,0,1:T(8,128)S(1)}, u32[]{:S(2)}) copy-start(f32[128,16,128]{2,0,1:T(8,128)S(1)} %copy.57) | copy-start | bytes 3145732
  6.4 1.0 copy-start.12
  169.4 70.1 %copy-start.18 = (f32[128,16,6]{0,1,2:T(8,128)S(1)}, f32[128,16,6]{0,1,2:T(8,128)}, u32[]{:S(2)}) copy-start(f32[128,16,6]{0,1,2:T(8,128)} %param.16) | copy-start | bytes 147460
  171.6 38.7 %collective-permute-start = (f32[16,128,128]{2,1,0:T(8,128)}, f32[16,128,128]{2,1,0:T(8,128)}, u32[]{:S(2)}, u32[]{:S(2)}) collective-permute-start(f32[16,128,128]{2,1,0:T(8,128)} %fusion.63), channel_id=1, source_target_pairs={{0,8},{8,0},{16,24},{24,16},{32,40},{40,32},{48,56},{56,48},{64,72... | collective-permute-start | bytes 3145736 | tf_op jit(solution)/shard_map/ppermute | solution.py:13
  173.1 23.7 %collective-permute-start.1 = (f32[16]{0:T(128)S(1)}, f32[16]{0:T(128)S(1)}, u32[]{:S(2)}, u32[]{:S(2)}) collective-permute-start(f32[16]{0:T(128)S(1)} %slice_reduce_fusion), channel_id=1, source_target_pairs={{0,8},{8,0},{16,24},{24,16},{32,40},{40,32},{48,56},{56,48},{64,72... | collective-permute-start | bytes 200 | tf_op jit(solution)/shard_map/ppermute | solution.py:13
  196.8 5.1 collective-permute-start.3
  201.9 3.6 collective-permute-start.5
  205.5 4.8 collective-permute-start.7
  212.2 22.9 %collective-permute-start.2 = (f32[16,128,128]{2,1,0:T(8,128)S(1)}, f32[16,128,128]{2,1,0:T(8,128)S(1)}, u32[]{:S(2)}, u32[]{:S(2)}) collective-permute-start(f32[16,128,128]{2,1,0:T(8,128)S(1)} %add_select_fusion.4), channel_id=1, source_target_pairs={{0,16},{8,24},{16,0},{24,8},{32,48},{40,56},{48,32},{56,40},{64,80... | collective-permute-start | bytes 3145736 | tf_op jit(solution)/shard_map/ppermute | solution.py:13
  235.1 1.4 copy-start.15
  235.1 27.4 %copy-start.19 = (f32[64,128]{1,0:T(8,128)S(1)}, f32[64,128]{1,0:T(8,128)}, u32[]{:S(2)}) copy-start(f32[64,128]{1,0:T(8,128)} %param.19) | copy-start | bytes 98308
  236.5 21.6 %collective-permute-start.4 = (f32[16,128,128]{2,1,0:T(8,128)}, f32[16,128,128]{2,1,0:T(8,128)}, u32[]{:S(2)}, u32[]{:S(2)}) collective-permute-start(f32[16,128,128]{2,1,0:T(8,128)} %add_select_fusion.3), channel_id=1, source_target_pairs={{0,32},{8,40},{16,48},{24,56},{32,0},{40,8},{48,16},{56,24},{64,96... | collective-permute-start | bytes 3145736 | tf_op jit(solution)/shard_map/ppermute | solution.py:13
  259.9 48.2 %copy-start.16 = (f32[16,128,128]{2,1,0:T(8,128)S(1)}, f32[16,128,128]{2,1,0:T(8,128)}, u32[]{:S(2)}) copy-start(f32[16,128,128]{2,1,0:T(8,128)} %copy-done.15) | copy-start | bytes 3145732
  259.9 41.7 %collective-permute-start.6 = (f32[16,128,128]{2,1,0:T(8,128)S(1)}, f32[16,128,128]{2,1,0:T(8,128)S(1)}, u32[]{:S(2)}, u32[]{:S(2)}) collective-permute-start(f32[16,128,128]{2,1,0:T(8,128)S(1)} %add_select_fusion.2), channel_id=1, source_target_pairs={{0,64},{8,72},{16,80},{24,88},{32,96},{40,104},{48,112},{56,120},{... | collective-permute-start | bytes 3145736 | tf_op jit(solution)/shard_map/ppermute | solution.py:13
  264.6 96.6 %copy-start.4 = (f32[16,128,128]{2,1,0:T(8,128)}, f32[16,128,128]{2,1,0:T(8,128)S(1)}, u32[]{:S(2)}) copy-start(f32[16,128,128]{2,1,0:T(8,128)S(1)} %convolution_multiply_fusion.1) | copy-start | bytes 3145732
  301.9 50.8 %collective-permute-start.8 = (f32[16,128,128]{2,1,0:T(8,128)S(1)}, f32[16,128,128]{2,1,0:T(8,128)S(1)}, u32[]{:S(2)}, u32[]{:S(2)}) collective-permute-start(f32[16,128,128]{2,1,0:T(8,128)S(1)} %add_select_fusion.1), channel_id=1, source_target_pairs={{0,128},{8,136},{16,144},{24,152},{32,160},{40,168},{48,176},{56,1... | collective-permute-start | bytes 3145736 | tf_op jit(solution)/shard_map/ppermute | solution.py:13
  361.2 1.9 copy-start.3
  361.2 1.9 copy-start.21
  363.9 123.4 %copy-start = (f32[16,128,128]{1,2,0:T(8,128)}, f32[16,128,128]{1,2,0:T(8,128)S(1)}, u32[]{:S(2)}) copy-start(f32[16,128,128]{1,2,0:T(8,128)S(1)} %get-tuple-element.25) | copy-start | bytes 3145732
  371.9 108.8 %copy-start.2 = (f32[5,16,128,128]{3,2,1,0:T(8,128)}, f32[5,16,128,128]{3,2,1,0:T(8,128)S(1)}, u32[]{:S(2)}) copy-start(f32[5,16,128,128]{3,2,1,0:T(8,128)S(1)} %fusion.8) | copy-start | bytes 15728644
  372.1 41.9 %collective-permute-start.10 = (f32[16,128,128]{2,1,0:T(8,128)S(1)}, f32[16,128,128]{2,1,0:T(8,128)S(1)}, u32[]{:S(2)}, u32[]{:S(2)}) collective-permute-start(f32[16,128,128]{2,1,0:T(8,128)S(1)} %fusion.48), channel_id=1, source_target_pairs={{0,128},{8,136},{16,144},{24,152},{32,160},{40,168},{48,176},{56,1... | collective-permute-start | bytes 3145736 | tf_op jit(solution)/shard_map/ppermute | solution.py:13
  375.6 38.3 %collective-permute-start.9 = (f32[16]{0:T(128)S(1)}, f32[16]{0:T(128)S(1)}, u32[]{:S(2)}, u32[]{:S(2)}) collective-permute-start(f32[16]{0:T(128)S(1)} %get-tuple-element.31), channel_id=1, source_target_pairs={{0,128},{8,136},{16,144},{24,152},{32,160},{40,168},{48,176},{56,1... | collective-permute-start | bytes 200 | tf_op jit(solution)/shard_map/ppermute | solution.py:13
  414.4 35.3 %collective-permute-start.11 = (f32[16,128,128]{2,1,0:T(8,128)S(1)}, f32[16,128,128]{2,1,0:T(8,128)S(1)}, u32[]{:S(2)}, u32[]{:S(2)}) collective-permute-start(f32[16,128,128]{2,1,0:T(8,128)S(1)} %fusion.45), channel_id=1, source_target_pairs={{0,64},{8,72},{16,80},{24,88},{32,96},{40,104},{48,112},{56,120},{... | collective-permute-start | bytes 3145736 | tf_op jit(solution)/shard_map/ppermute | solution.py:13
  451.3 36.1 %copy-start.11 = (f32[16,128,128]{2,1,0:T(8,128)}, f32[16,128,128]{2,1,0:T(8,128)S(1)}, u32[]{:S(2)}) copy-start(f32[16,128,128]{2,1,0:T(8,128)S(1)} %get-tuple-element.29) | copy-start | bytes 3145732
  451.3 29.3 %collective-permute-start.12 = (f32[16,128,128]{2,1,0:T(8,128)S(1)}, f32[16,128,128]{2,1,0:T(8,128)S(1)}, u32[]{:S(2)}, u32[]{:S(2)}) collective-permute-start(f32[16,128,128]{2,1,0:T(8,128)S(1)} %get-tuple-element.28), channel_id=1, source_target_pairs={{0,32},{8,40},{16,48},{24,56},{32,0},{40,8},{48,16},{56,24},{64,96... | collective-permute-start | bytes 3145736 | tf_op jit(solution)/shard_map/ppermute | solution.py:13
  459.4 25.7 %copy-start.6 = (f32[16,128,128]{2,1,0:T(8,128)}, f32[16,128,128]{2,1,0:T(8,128)S(1)}, u32[]{:S(2)}) copy-start(f32[16,128,128]{2,1,0:T(8,128)S(1)} %convolution_multiply_fusion) | copy-start | bytes 3145732
  480.6 12.8 %copy-start.14 = (f32[16,128,128]{2,1,0:T(8,128)}, f32[16,128,128]{2,1,0:T(8,128)S(1)}, u32[]{:S(2)}) copy-start(f32[16,128,128]{2,1,0:T(8,128)S(1)} %collective-permute-done.12) | copy-start | bytes 3145732
  482.0 93.4 %collective-permute-start.13 = (f32[16,128,128]{2,1,0:T(8,128)}, f32[16,128,128]{2,1,0:T(8,128)}, u32[]{:S(2)}, u32[]{:S(2)}) collective-permute-start(f32[16,128,128]{2,1,0:T(8,128)} %fusion.39), channel_id=1, source_target_pairs={{0,16},{8,24},{16,0},{24,8},{32,48},{40,56},{48,32},{56,40},{64,80... | collective-permute-start | bytes 3145736 | tf_op jit(solution)/shard_map/ppermute | solution.py:13
  575.5 4.0 copy-start.1
  575.5 4.0 copy-start.5
  575.5 5.9 copy-start.7
  578.3 15.3 %collective-permute-start.14 = (f32[16,128,128]{2,1,0:T(8,128)S(1)}, f32[16,128,128]{2,1,0:T(8,128)S(1)}, u32[]{:S(2)}, u32[]{:S(2)}) collective-permute-start(f32[16,128,128]{2,1,0:T(8,128)S(1)} %get-tuple-element.26), channel_id=1, source_target_pairs={{0,8},{8,0},{16,24},{24,16},{32,40},{40,32},{48,56},{56,48},{64,72... | collective-permute-start | bytes 3145736 | tf_op jit(solution)/shard_map/ppermute | solution.py:13
  581.4 16.5 %copy-start.9 = (f32[128,16,128]{2,0,1:T(8,128)S(1)}, f32[128,16,128]{2,0,1:T(8,128)}, u32[]{:S(2)}) copy-start(f32[128,16,128]{2,0,1:T(8,128)} %copy-done.8) | copy-start | bytes 3145732
  581.4 16.5 %copy-start.10 = (f32[16,1,128,128]{2,3,1,0:T(8,128)S(1)}, f32[16,1,128,128]{2,3,1,0:T(8,128)}, u32[]{:S(2)}) copy-start(f32[16,1,128,128]{2,3,1,0:T(8,128)} %custom-call.7) | copy-start | bytes 3145732
  593.6 5.9 copy-start.13
where the time goes:
time: 622 us; the launch traced here: 613 us
  waiting for transfers between devices  246 us (40%)
  other arithmetic  178 us (29%)
  blocking collectives  79 us (13%)
  matrix products  54.6 us (9%)
  starting transfers between devices  39.7 us (6%)
  local copies, waits for them, and re-layouts  13.7 us (2%)
    ppermute x15, waiting for transfers between devices, from_partner(): return lax.ppermute(value, axis, pairs)  246 us
    another operation x2, other arithmetic, prepare(): jax.scipy.linalg.solve_triangular(system, beta_heads[:, :, None] * value_...  159 us
    psum x1, blocking collectives, local(): grad_gain = lax.psum(grad_gain_local, 'ctx')  79 us
    ppermute x15, starting transfers between devices, from_partner(): return lax.ppermute(value, axis, pairs)  39.7 us
    dot_general x3, matrix products, finish(): jnp.einsum('htk,lhkv->lhtv', query_normed, bucket_states, precision=topmo...  20.6 us
  transfers between devices with their start and end apart: 15, of which 12 were waited for; matrix products, arithmetic and copies ran while one was open for 4% of the time, Pallas kernels for 0%

commit v1 on v0

v1 whole, which is shorter than its diff:
```python
import jax
import jax.numpy as jnp
from jax import lax
from jax.experimental import pallas as pl
from jax.experimental.pallas import tpu as pltpu
from jax.sharding import PartitionSpec as P


EPS = 1e-06
F32 = jnp.float32
BF16 = jnp.bfloat16
N = 128
HALF = 64
GROUP = 4
LEVELS = 5
INTERPRET = False

NN = ((1,), (0,))
NT = ((1,), (1,))
TN = ((0,), (0,))


def dot(a, b, dims):
    return lax.dot_general(a, b, (dims, ((), ())), preferred_element_type=F32)


def split(a):
    hi = a.astype(BF16)
    return hi, (a - hi.astype(F32)).astype(BF16)


def cat(parts, axis):
    return jnp.concatenate(parts, axis=axis)


def dot_left(a, b, dims=NN):
    hi, lo = split(a)
    ca, cb = dims[0][0], dims[1][0]
    return dot(cat([hi, lo], ca), cat([b, b], cb), dims)


def dot_split(a, b, dims=NN):
    ca, cb = dims[0][0], dims[1][0]
    return dot(cat([a[0], a[1]], ca), cat([b[0], b[0]], cb), dims) + dot(a[0], b[1], dims)


def dot_full(a, b, dims=NN):
    return dot_split(split(a), split(b), dims)


def iotas():
    return (
        lax.broadcasted_iota(jnp.int32, (N, N), 0),
        lax.broadcasted_iota(jnp.int32, (N, N), 1),
    )


def inv_norm_col(raw):
    return lax.rsqrt(jnp.sum(raw * raw, axis=1, keepdims=True) + EPS)


def unit_lower_inverse(lowers, mask_ref):
    row16 = lax.broadcasted_iota(jnp.int32, (16, N), 0)
    col16 = lax.broadcasted_iota(jnp.int32, (16, N), 1)
    base = col16 & 112
    start = jnp.where((col16 & 15) == row16, 1.0, 0.0).astype(F32)
    packed = [(a * mask_ref[1]).reshape(8, 16, N).sum(axis=0) for a in lowers]
    inverses = [start for _ in lowers]
    for j in range(15):
        index = base | j
        for h, rows in enumerate(packed):
            column = jnp.take_along_axis(rows, index, axis=1, mode="promise_in_bounds")
            inverses[h] = inverses[h] - column * inverses[h][j : j + 1, :]
    inverses = [jnp.broadcast_to(a[None], (8, 16, N)).reshape(N, N) * mask_ref[1] for a in inverses]
    for level in range(3):
        pairs = [split(a) for a in inverses]
        inner = [dot_split(split(a * mask_ref[2 + level]), p) for a, p in zip(lowers, pairs)]
        inverses = [a - dot_split(p, split(c)) for a, p, c in zip(inverses, pairs, inner)]
    return inverses


def fill_masks(mask_ref):
    row, col = iotas()
    mask_ref[0] = jnp.where(row > col, 0.0, -1e30)
    mask_ref[1] = jnp.where((row >> 4) == (col >> 4), 1.0, 0.0)
    for level in range(3):
        bits = 4 + level
        below = ((row >> bits) & 1 == 1) & ((col >> bits) == (row >> bits) - 1)
        mask_ref[2 + level] = jnp.where(below, 1.0, 0.0)
    mask_ref[5] = jnp.where(row == col, 1.0, 0.0)


def token_sums(gate_ref, beta_ref, cols_ref, rows_ref, total_ref):
    row, col = iotas()
    gate = gate_ref[...]
    beta = beta_ref[...]
    upper = jnp.where(row <= col, 1.0, 0.0).astype(BF16)
    hi, lo = split(gate)
    rest = (gate - hi.astype(F32) - lo.astype(F32)).astype(BF16)
    cum = dot(cat([hi, lo, rest], 1), cat([upper] * 3, 0), NN)
    total_ref[...] = jnp.broadcast_to(cum[:, N - 1 : N], cum.shape)
    columns = cat([cum, beta], 0).T
    for s in range(4):
        part = slice(s * GROUP, (s + 1) * GROUP)
        rows_ref[s] = cat([cum[part], beta[part]], 0)
        cols_ref[s] = cat([columns[:, part], columns[:, 16 + s * GROUP : 16 + (s + 1) * GROUP]], 1)


def solve_kernel(
    x_ref, gate_ref, beta_ref, key_ref, value_ref,
    r0_ref, r1_ref, r2_ref, r3_ref, s0_ref, s1_ref,
    pseudo_ref, inv_ref, norm_ref, cols_ref, rows_ref, total_ref, mask_ref, gather_ref,
):
    ring_refs = r0_ref, r1_ref, r2_ref, r3_ref
    half_refs = s0_ref, s1_ref
    step = pl.program_id(0)
    x = x_ref[0]

    @pl.when(step == 0)
    def _():
        fill_masks(mask_ref)
        token_sums(gate_ref, beta_ref, cols_ref, rows_ref, total_ref)

    cols = cols_ref[step]
    rows = rows_ref[step]

    group = range(GROUP)
    kb = [key_ref[:, j * N : (j + 1) * N] for j in group]
    inner = [dot(k, k, NT) for k in kb]
    lowers, rk_cols = [], []
    for j in group:
        diagonal = inner[j] * mask_ref[5]
        rk_row = lax.rsqrt(jnp.sum(diagonal, axis=0, keepdims=True) + EPS)
        rk_cols.append(lax.rsqrt(jnp.sum(diagonal, axis=1, keepdims=True) + EPS))
        norm_ref[0, j : j + 1, :] = rk_row
        decay = jnp.exp((cols[:, j : j + 1] - rows[j : j + 1]) + mask_ref[0])
        lowers.append((cols[:, GROUP + j : GROUP + j + 1] * rk_cols[j]) * (decay * (rk_row * inner[j])))
    inverses = unit_lower_inverse(lowers, mask_ref)
    for j in group:
        inv_ref[j] = inverses[j]
    pseudos = [
        dot_left(inverses[j] * rows[GROUP + j : GROUP + j + 1], value_ref[:, j * N : (j + 1) * N])
        for j in group
    ]
    states = []
    for j in group:
        pseudo_ref[j] = pseudos[j]
        trailing = jnp.exp(rows[j : j + 1, N - 1 : N] - cols[:, j : j + 1]) * rk_cols[j]
        hi, lo = split(pseudos[j] * trailing)
        states.append(dot(cat([kb[j], kb[j]], 0), cat([hi, lo], 0), TN))
    for j in group:
        for half in range(2):
            rows = slice((j >> 1) * HALF, (j >> 1) * HALF + HALF)
            gather_ref[2 * (j & 1) + half, rows, :] = states[j][half * HALF : (half + 1) * HALF]
    base = pl.multiple_of(step * N, N)
    for slot in range(4):
        part = gather_ref[x ^ slot]
        ring_refs[slot][pl.ds(base, N), :] = part
        half_refs[slot >> 1][slot & 1] = part

    @pl.when(step == pl.num_programs(0) - 1)
    def _():
        for slot in range(4):
            ring_refs[slot][4 * N : 4 * N + 16, :] = total_ref[...]


def intra_kernel(query_ref, key_ref, cols_ref, rows_ref, norm_ref, pseudo_ref, intra_ref):
    row, col = iotas()
    group = range(GROUP)
    qb = [query_ref[:, j * N : (j + 1) * N] for j in group]
    products = [dot(qb[j], key_ref[:, j * N : (j + 1) * N], NT) for j in group]
    penalty = jnp.where(row >= col, 0.0, -1e30)
    scores = []
    for j in group:
        rq_col = inv_norm_col(qb[j].astype(F32))
        decay = jnp.exp((cols_ref[0, :, j : j + 1] - rows_ref[0, j : j + 1, :]) + penalty)
        scores.append(rq_col * (products[j] * norm_ref[0, j : j + 1, :]) * decay)
    for j in group:
        intra_ref[j] = dot_full(scores[j], pseudo_ref[j])


def place_pieces(x, pieces, scratch_ref):
    for level in range(3):
        for m in range(4):
            scratch_ref[level, x ^ m] = pieces[4 * level + m][...]


def from_halves(refs, slot, rows):
    return jnp.where(slot < 2, refs[0][slot & 1, rows, :], refs[1][slot & 1, rows, :])


def bucket_of(x, j, level, near_refs, pair_refs, scratch_ref):
    rows = slice((j >> 1) * HALF, (j >> 1) * HALF + HALF)
    parts = []
    for half in range(2):
        quarter = 2 * (j & 1) + half
        if level == 0:
            parts.append(from_halves(near_refs, (x ^ 1) ^ quarter, rows))
        elif level == 1:
            parts.append(from_halves(pair_refs, (x ^ 3) ^ quarter, rows))
        else:
            parts.append(scratch_ref[level - 2, quarter, rows, :])
    return cat(parts, 0)


def cross_kernel(*refs):
    x_ref, query_ref, out_ref, intra_ref, weight_ref, gain_ref = refs[:6]
    near_refs, pair_refs, pieces = refs[6:8], refs[8:10], refs[10:22]
    g1_ref, g2_refs = refs[22], refs[23:25]
    g34_refs, g5_refs = refs[25:29], refs[29:33]
    dm_ref, level_ref = refs[33:35]
    scratch_ref, gather_ref, gain_sum_ref = refs[35:38]
    step = pl.program_id(0)
    x = x_ref[0]
    group = range(GROUP)
    place_pieces(x, pieces, scratch_ref)
    gain = gain_ref[...]
    lane = lax.broadcasted_iota(jnp.int32, (N, 8 * GROUP), 1)
    gain_sum = jnp.zeros((8, N), F32)
    weights = weight_ref[0].T
    levels = jnp.zeros((N, 8 * GROUP), F32)
    qb = [query_ref[:, j * N : (j + 1) * N] for j in group]
    crosses = []
    for j in group:
        pairs = [split(bucket_of(x, j, level, near_refs, pair_refs, scratch_ref)) for level in range(LEVELS)]
        right = cat([cat([p[0] for p in pairs], 1), cat([p[1] for p in pairs], 1)], 0)
        crosses.append(dot(cat([qb[j], qb[j]], 1), right, NN))
    lefts = []
    for j in group:
        go = out_ref[:, j * N : (j + 1) * N].astype(F32)
        rq_col = inv_norm_col(qb[j].astype(F32))
        scaled_weights = weights * jnp.where(lane < GROUP, 1.0, rq_col)
        columns = [
            jnp.broadcast_to(scaled_weights[:, l * GROUP + j : l * GROUP + j + 1], (N, N)) for l in range(LEVELS + 1)
        ]
        intra = intra_ref[j]
        mixture = columns[0] * intra
        for level in range(LEVELS):
            mixture = mixture + columns[level + 1] * crosses[j][:, level * N : (level + 1) * N]
        inverse_rms = lax.rsqrt(jnp.mean(mixture * mixture, axis=1, keepdims=True) + EPS)
        scaled = mixture * inverse_rms
        gain_sum = gain_sum + (go * scaled).reshape(N // 8, 8, N).sum(axis=0)
        dn = go * gain
        dm = inverse_rms * (dn - scaled * jnp.mean(dn * scaled, axis=1, keepdims=True))
        dm_ref[j] = dm
        levels = jnp.where(lane == j, jnp.sum(dm * intra, axis=1, keepdims=True), levels)
        pairs = []
        for level in range(LEVELS):
            along = jnp.sum(dm * crosses[j][:, level * N : (level + 1) * N], axis=1, keepdims=True) * rq_col
            levels = jnp.where(lane == (level + 1) * GROUP + j, along, levels)
            pairs.append(split(dm * columns[level + 1]))
        lefts.append(cat([cat([p[0] for p in pairs], 1), cat([p[1] for p in pairs], 1)], 0))
    level_ref[0] = levels.T
    for j in group:
        grads = dot(cat([qb[j], qb[j]], 0), lefts[j], TN)
        rows = slice((j >> 1) * HALF, (j >> 1) * HALF + HALF)
        for half in range(2):
            quarter = 2 * (j & 1) + half
            part = grads[half * HALF : (half + 1) * HALF]
            g1_ref[x ^ quarter, rows, :] = part[:, 0:N]
            for level in range(4):
                gather_ref[level, quarter, rows, :] = part[:, (1 + level) * N : (2 + level) * N]
    base = pl.multiple_of(step * N, N)
    for m in range(4):
        g2_refs[m >> 1][m & 1] = gather_ref[0, x ^ m]
        for level in range(2):
            g34_refs[2 * level + (m in (1, 2))][m >> 1] = gather_ref[1 + level, x ^ m]
        g5_refs[m][pl.ds(base, N), :] = gather_ref[3, x ^ m]

    @pl.when(step == 0)
    def _():
        gain_sum_ref[...] = jnp.zeros((8, N), F32)

    gain_sum_ref[...] += gain_sum

    @pl.when(step == pl.num_programs(0) - 1)
    def _():
        for m in range(4):
            g5_refs[m][4 * N : 4 * N + 8, :] = gain_sum_ref[...]


def query_kernel(*refs):
    x_ref, query_ref, key_ref, cols_ref, rows_ref, norm_ref, weight_ref, pseudo_ref, dm_ref = refs[:9]
    near_refs, pair_refs, pieces = refs[9:11], refs[11:13], refs[13:25]
    gq_ref, dp_ref, dk_ref, scratch_ref, mask_ref = refs[25:30]
    x = x_ref[0]
    group = range(GROUP)

    @pl.when(pl.program_id(0) == 0)
    def _():
        row, col = iotas()
        mask_ref[...] = jnp.where(row >= col, 0.0, -1e30)

    place_pieces(x, pieces, scratch_ref)
    qb = [query_ref[:, j * N : (j + 1) * N] for j in group]
    kb = [key_ref[:, j * N : (j + 1) * N] for j in group]
    products = [dot(q, k, NT) for q, k in zip(qb, kb)]
    weights = weight_ref[0].T
    owns = [split(dm_ref[j] * weights[:, j : j + 1]) for j in group]
    dscores = [dot_split(owns[j], split(pseudo_ref[j]), NT) for j in group]
    dqs, rqs = [], []
    for j in group:
        rq_col = inv_norm_col(qb[j].astype(F32))
        rqs.append(rq_col)
        rk_row = norm_ref[0, j : j + 1, :]
        decay = jnp.exp((cols_ref[0, :, j : j + 1] - rows_ref[0, j : j + 1, :]) + mask_ref[...])
        scores = rq_col * (products[j] * rk_row) * decay
        dscore = dscores[j] * decay
        dp_ref[j] = dot_split(split(scores), owns[j], TN)
        dqs.append(dot_left(dscore * rk_row, kb[j]))
        hi, lo = split(dscore * rq_col)
        dk_ref[j] = dot(cat([hi, lo], 0), cat([qb[j], qb[j]], 0), TN)
    for j in group:
        dm = dm_ref[j]
        lefts = [split(dm * weights[:, (level + 1) * GROUP + j : (level + 1) * GROUP + j + 1]) for level in range(LEVELS)]
        rights = [split(bucket_of(x, j, level, near_refs, pair_refs, scratch_ref)) for level in range(LEVELS)]
        left = cat([p[0] for p in lefts], 1), cat([p[1] for p in lefts], 1)
        right = cat([p[0] for p in rights], 1), cat([p[1] for p in rights], 1)
        dqs[j] = dqs[j] + dot_split(left, right, NT)
    for j in group:
        qf = qb[j].astype(F32)
        along = jnp.sum(dqs[j] * qf, axis=1, keepdims=True)
        gq_ref[:, j * N : (j + 1) * N] = (rqs[j] * (dqs[j] - qf * (rqs[j] * rqs[j] * along))).astype(BF16)


def final_kernel(
    x_ref, key_ref, value_ref, cols_ref, rows_ref, norm_ref, coef_ref, inv_ref, pseudo_ref, dp_ref, dk_ref,
    p0_ref, p1_ref, n0_ref, n1_ref, a0_ref, a1_ref, a2_ref, a3_ref, gk_ref, gv_ref, gb_ref, scratch_ref, mask_ref,
):
    x = x_ref[0]
    group = range(GROUP)

    @pl.when(pl.program_id(0) == 0)
    def _():
        row, col = iotas()
        mask_ref[...] = jnp.where(row > col, 0.0, -1e30)

    for m, ref in enumerate((a0_ref, a1_ref, a2_ref, a3_ref)):
        scratch_ref[x ^ m] = ref[...]
    kb = [key_ref[:, j * N : (j + 1) * N] for j in group]
    gs, rk_cols, trailings, decays, pseudos = [], [], [], [], []
    for j in group:
        rows = slice((j >> 1) * HALF, (j >> 1) * HALF + HALF)
        parts = []
        for half in range(2):
            quarter = 2 * (j & 1) + half
            parts.append(
                coef_ref[0, 0, j : j + 1, :] * from_halves((p0_ref, p1_ref), (x ^ 3) ^ quarter, rows)
                + from_halves((n0_ref, n1_ref), (x ^ 1) ^ quarter, rows)
                + coef_ref[1, 0, j : j + 1, :] * scratch_ref[quarter, rows, :]
            )
        gs.append(split(cat(parts, 0)))
    ups = [dot(cat([kb[j], kb[j]], 1), cat([gs[j][0], gs[j][1]], 0), NN) for j in group]
    inners = [dot(k, k, NT) for k in kb]
    dps = []
    for j in group:
        rk_cols.append(inv_norm_col(kb[j].astype(F32)))
        cum_col = cols_ref[0, :, j : j + 1]
        cum_row = rows_ref[0, j : j + 1, :]
        trailings.append(jnp.exp(cum_row[:, N - 1 : N] - cum_col))
        decays.append(jnp.exp((cum_col - cum_row) + mask_ref[...]))
        dps.append(split(dp_ref[j] + (trailings[j] * rk_cols[j]) * ups[j]))
    dxs = [dot_split(split(inv_ref[j]), dps[j], TN) for j in group]
    pseudos = [split(pseudo_ref[j]) for j in group]
    dks = [dk_ref[j] + trailings[j] * dot_split(pseudos[j], gs[j], NT) for j in group]
    das = [dot_split(split(dxs[j]), pseudos[j], NT) for j in group]
    backs, fronts = [], []
    lane = lax.broadcasted_iota(jnp.int32, (N, 8), 1)
    grad_beta = jnp.zeros((N, 8), F32)
    for j in group:
        vf = value_ref[:, j * N : (j + 1) * N].astype(F32)
        rk_row = norm_ref[0, j : j + 1, :]
        beta_col = cols_ref[0, :, GROUP + j : GROUP + j + 1]
        gv_ref[:, j * N : (j + 1) * N] = (beta_col * dxs[j]).astype(BF16)
        da = das[j] * decays[j]
        along = jnp.sum(dxs[j] * vf - rk_cols[j] * (da * (rk_row * inners[j])), axis=1, keepdims=True)
        grad_beta = jnp.where(lane == j, along, grad_beta)
        da = da * beta_col
        fronts.append(dot_left(da * rk_row, kb[j]))
        hi, lo = split(da * rk_cols[j])
        backs.append(dot(cat([hi, lo], 0), cat([kb[j], kb[j]], 0), TN))
    gb_ref[0] = grad_beta.T
    for j in group:
        kf = kb[j].astype(F32)
        dk = dks[j] - fronts[j] - backs[j]
        along = jnp.sum(dk * kf, axis=1, keepdims=True)
        gk_ref[:, j * N : (j + 1) * N] = (rk_cols[j] * (dk - kf * (rk_cols[j] * rk_cols[j] * along))).astype(BF16)


def call(kernel, prefetch, ins, in_specs, outs, out_specs, scratch=()):
    heads = 16
    grid_spec = pltpu.PrefetchScalarGridSpec(
        num_scalar_prefetch=len(prefetch),
        grid=(heads // GROUP,),
        in_specs=in_specs,
        out_specs=out_specs,
        scratch_shapes=list(scratch),
    )
    return pl.pallas_call(
        kernel,
        grid_spec=grid_spec,
        out_shape=outs,
        interpret=INTERPRET,
        compiler_params=pltpu.CompilerParams(dimension_semantics=("arbitrary",)),
    )(*prefetch, *ins)


def spec(shape, index):
    return pl.BlockSpec(shape, lambda i, *_: index(i))


TOKENS = spec((N, GROUP * N), lambda i: (0, i))
COLS = spec((1, N, 8), lambda i: (i, 0, 0))
WEIGHTS = spec((1, 8 * GROUP, N), lambda i: (i, 0, 0))
ROWS = spec((1, 8, N), lambda i: (i, 0, 0))
NORMS = spec((1, GROUP, N), lambda i: (i, 0, 0))
SQUARE = spec((GROUP, N, N), lambda i: (i, 0, 0))
SLOTS = spec((4, N, N), lambda i: (0, i, 0))
PAIRS = spec((2, N, N), lambda i: (0, i, 0))
PIECE = spec((N, N), lambda i: (i, 0))


def shape(*dims, dtype=F32):
    return jax.ShapeDtypeStruct(dims, dtype)


def permute(value, flip, only=None):
    size = lax.axis_size("ctx")
    pairs = [(s, s ^ flip) for s in range(size) if only is None or (s & 3) in only]
    return lax.ppermute(value, "ctx", pairs)


def block(query, key, value, beta, log_gate, level_weight, norm_gain, grad_out, grad_final_state):
    heads = beta.shape[1]
    device = lax.axis_index("ctx")
    x = device & 3
    z = device >> 2
    xs = jnp.reshape(x, (1,)).astype(jnp.int32)

    square = shape(heads, N, N)
    whole = spec((heads, N), lambda i: (0, 0))
    r0, r1, r2, r3, s0, s1, pseudo, inverse, norms, cols, rows, own_total = call(
        solve_kernel, (xs,), (log_gate.T, beta.T, key, value),
        [whole, whole, TOKENS, TOKENS],
        [shape(4 * N + 16, N)] * 4 + [shape(2, 4 * N, N)] * 2
        + [square, square, shape(4, GROUP, N), shape(4, N, 8), shape(4, 8, N), shape(heads, N)],
        [spec((4 * N + 16, N), lambda i: (0, 0))] * 4 + [PAIRS] * 2 + [SQUARE, SQUARE, NORMS]
        + [spec((4, N, 8), lambda i: (0, 0, 0)), spec((4, 8, N), lambda i: (0, 0, 0)), whole],
        scratch=[pltpu.VMEM((6, N, N), F32), pltpu.VMEM((4, N, N), F32)],
    )

    def pick(tile):
        pairs = tile.reshape(8, 2, N)
        return jnp.where(x >= 2, pairs[:, 1], pairs[:, 0])[:, None, :]

    def quarter(rows_):
        return rows_[: 4 * N].reshape(8, HALF, N)

    gathered = [r0] + [permute(r, m) for m, r in ((1, r1), (2, r2), (3, r3))]
    totals = [own_total] + [g[4 * N :] for g in gathered[1:]]
    nears = [permute(s, 1, only=(0, 1, 2)) for s in (s0, s1)]
    after = []
    for m in range(4):
        after.append(sum(jnp.where((x ^ k) > (x ^ m), totals[k], 0.0) for k in range(4) if k != m))
    before = sum(jnp.where((x ^ k) < x, totals[k], 0.0) for k in range(1, 4))
    group_total = sum(totals)
    aggregate = sum(jnp.exp(pick(after[m])) * quarter(gathered[m]) for m in range(4))

    intra = call(
        intra_kernel, (), (query, key, cols, rows, norms, pseudo),
        [TOKENS, TOKENS, COLS, ROWS, NORMS, SQUARE], square, SQUARE,
    )

    omegas = [
        jnp.where(x & 1 == 1, jnp.ones((heads, N), F32), 0.0),
        jnp.where(x >= 2, jnp.exp(jnp.where(x & 1 == 1, totals[1], 0.0)), 0.0),
    ]
    records = []
    pieces = []
    offset = before
    pairs = []
    for degree, flip in enumerate((1, 2, 7)):
        upper = (z >> degree) & 1 == 1
        payload = cat([aggregate.reshape(4 * N, N), group_total], 0)
        received = permute(payload, flip << 2)
        if degree == 0:
            decays = totals[1].reshape(8, 2, N), own_total.reshape(8, 2, N)
            keep, take = (jnp.exp(d).transpose(1, 0, 2)[:, None, :, None, :] for d in decays)
            keep = jnp.where(x == 0, keep, 1.0)
            take = jnp.where(x == 0, 1.0, take)
            for k, own in enumerate((s0, s1)):
                other = nears[k].reshape(2, 8, HALF, N)[::-1]
                payload = keep[k] * own.reshape(2, 8, HALF, N) + take[k] * other
                pairs.append(permute(payload.reshape(2, 4 * N, N), 3, only=(0, 1)))
        partner_total = received[4 * N :]
        omegas.append(jnp.where(upper, jnp.exp(offset), 0.0))
        records.append((upper, group_total, partner_total))
        third = permute(received, 3)
        first = permute(received, 1)
        second = permute(received, 2) if degree > 0 else permute(third, 1)
        pieces += [received, first, second, third]
        aggregate = jnp.where(
            upper,
            jnp.exp(pick(group_total)) * quarter(received) + aggregate,
            jnp.exp(pick(partner_total)) * aggregate + quarter(received),
        )
        offset = jnp.where(upper, offset + partner_total, offset)
        group_total = group_total + partner_total
    final_state = lax.dynamic_index_in_dim(aggregate, z, 0, keepdims=False)
    growth = jnp.exp(rows[:, :GROUP].reshape(1, heads, N)) * jnp.stack(omegas)
    growth = cat([jnp.ones((1, heads, N), F32), growth], 0)
    weights = jnp.pad(level_weight.transpose(2, 1, 0) * growth, ((0, 2), (0, 0), (0, 0)))
    weights = weights.reshape(8, 4, GROUP, N).transpose(1, 0, 2, 3).reshape(4, 8 * GROUP, N)

    outs = call(
        cross_kernel, (xs,),
        (query, grad_out, intra, weights, norm_gain.reshape(1, N), *nears, *pairs, *pieces),
        [TOKENS, TOKENS, SQUARE, WEIGHTS, spec((1, N), lambda i: (0, 0))] + [PAIRS] * 4 + [PIECE] * 12,
        [shape(4, 4 * N, N)] + [shape(2, 4 * N, N)] * 6 + [shape(4 * N + 8, N)] * 4 + [square, shape(4, 8 * GROUP, N)],
        [SLOTS] + [PAIRS] * 6
        + [spec((4 * N + 8, N), lambda i: (0, 0))] * 4 + [SQUARE, WEIGHTS],
        scratch=[pltpu.VMEM((3, 4, N, N), F32), pltpu.VMEM((4, 4, N, N), F32), pltpu.VMEM((8, N), F32)],
    )
    grad_near, grad_pairs = outs[0], outs[1:3]
    grads34, grads5 = outs[3:7], outs[7:11]
    grad_mixture, grad_level_rows = outs[11:]

    top = grads5[0] + sum(permute(grads5[m], m) for m in range(1, 4))
    pair_backs = [permute(g, 3, only=(2, 3)) for g in grad_pairs]
    middle = []
    for level in range(2):
        kept, sent = grads34[2 * level : 2 * level + 2]
        first = permute(sent, 1)
        second = permute(kept[1] + first[1], 3)
        middle.append(kept[0] + first[0] + second)

    blocks = lax.broadcasted_iota(jnp.int32, (8, 1, 1), 0)
    adjoint = jnp.where(blocks == z, grad_final_state[None], 0.0)
    gain_rows = top[4 * N :]
    bucket_grads = [middle[0], middle[1], top[: 4 * N]]
    for degree, flip in ((2, 7), (1, 2), (0, 1)):
        upper, group_total, partner_total = records[degree]
        outgoing = quarter(bucket_grads[degree]) + jnp.where(upper, jnp.exp(pick(group_total)) * adjoint, adjoint)
        incoming = permute(cat([outgoing.reshape(4 * N, N), gain_rows], 0), flip << 2)
        adjoint = jnp.where(upper, adjoint, jnp.exp(pick(partner_total)) * adjoint) + quarter(incoming)
        gain_rows = gain_rows + incoming[4 * N :]
    adjoint = adjoint.reshape(4 * N, N)
    adjoints = [adjoint] + [permute(adjoint, m) for m in range(1, 4)]

    near_backs = []
    for k in range(2):
        back = pair_backs[1 - k].reshape(2, 8, HALF, N)[::-1]
        own = grad_near[2 * k : 2 * k + 2].reshape(2, 8, HALF, N)
        near_backs.append(permute((own + take[k] * back).reshape(2, 4 * N, N), 1, only=(0, 1, 3)))

    grad_query, grad_pseudo, grad_key_part = call(
        query_kernel, (xs,),
        (query, key, cols, rows, norms, weights, pseudo, grad_mixture, *nears, *pairs, *pieces),
        [TOKENS, TOKENS, COLS, ROWS, NORMS, WEIGHTS, SQUARE, SQUARE] + [PAIRS] * 4 + [PIECE] * 12,
        [shape(N, heads * N, dtype=BF16), square, square], [TOKENS, SQUARE, SQUARE],
        scratch=[pltpu.VMEM((3, 4, N, N), F32), pltpu.VMEM((N, N), F32)],
    )

    coef_pair = jnp.where(x < 2, jnp.exp(jnp.where(x == 0, totals[1], 0.0)), 0.0)
    coefs = jnp.stack([coef_pair, jnp.exp(after[0])]).reshape(2, 4, GROUP, N)
    grad_key, grad_value, grad_beta_rows = call(
        final_kernel, (xs,),
        (key, value, cols, rows, norms, coefs, inverse, pseudo, grad_pseudo, grad_key_part, *pair_backs, *near_backs, *adjoints),
        [TOKENS, TOKENS, COLS, ROWS, NORMS, spec((2, 1, GROUP, N), lambda i: (0, i, 0, 0))]
        + [SQUARE] * 4 + [PAIRS] * 4 + [PIECE] * 4,
        [shape(N, heads * N, dtype=BF16), shape(N, heads * N, dtype=BF16), shape(4, 8, N)],
        [TOKENS, TOKENS, ROWS],
        scratch=[pltpu.VMEM((4, N, N), F32), pltpu.VMEM((N, N), F32)],
    )
    return (
        grad_query,
        grad_key,
        grad_value,
        grad_beta_rows[:, :GROUP].reshape(heads, N).T,
        (grad_level_rows.reshape(4, 8, GROUP, N)[:, :6].transpose(1, 0, 2, 3).reshape(6, heads, N) * growth).transpose(2, 1, 0),
        gain_rows.sum(axis=0),
        final_state,
    )


def solution(mesh):
    tokens = P(("rep", "ctx"), None)
    levels = P(("rep", "ctx"), None, None)
    in_specs = (tokens, tokens, tokens, tokens, tokens, levels, P(), tokens, tokens)
    out_specs = (tokens, tokens, tokens, tokens, levels, P("rep"), tokens)
    return jax.shard_map(block, mesh=mesh, in_specs=in_specs, out_specs=out_specs, check_vma=False)
```

time: 622 us -> 221 us (0.36); the launches traced: 613 us -> 220 us
  other arithmetic: 178 us -> 8.88 us
  waiting for transfers between devices: 246 us -> 83.5 us
  blocking collectives: 79 us -> 0 us
  matrix products: 54.6 us -> 0 us
  Pallas kernels: 0 us -> 50.4 us
  starting transfers between devices: 39.7 us -> 66.1 us
    ppermute x15 -> x36, waiting for transfers between devices: 246 us -> 83.5 us  [permute(): return lax.ppermute(value, 'ctx', pairs)]
    another operation x4 -> x2, other arithmetic: 159 us -> 0.61 us  [the longest x1 0.6 us: block(): coefs = jnp.stack([coef_pair, jnp.exp(after[0])]).reshape(2, 4, GROUP, N)]
    psum x1 -> x0, blocking collectives: 79 us -> none  [local(): grad_gain = lax.psum(grad_gain_local, 'ctx')]
    pallas_call x0 -> x5, Pallas kernels: none -> 50.4 us  [call(): pl.pallas_call(kernel, grid_spec=grid_spec, out_shape=outs, interpret=INT...]
    dot_general x16 -> x0, matrix products: 47.1 us -> none  [the longest x3 20.6 us: finish(): jnp.einsum('htk,lhkv->lhtv', query_normed, bucket_states, precision=topmo...]
    ppermute x15 -> x36, starting transfers between devices: 39.7 us -> 66.1 us  [permute(): return lax.ppermute(value, 'ctx', pairs)]
    select_n x9 -> x1, other arithmetic: 11.7 us -> 0.86 us  [block(): jnp.where(upper, jnp.exp(pick(group_total)) * quarter(received) + aggrega...]
    another operation x3 -> x0, matrix products: 7.47 us -> none  [prepare(): jax.scipy.linalg.solve_triangular(system, beta_heads[:, :, None] * value_...]
  transfers between devices with their start and end apart: 15 -> 36, of which waited for: 12 -> 20; matrix products, arithmetic and copies ran while one was open for 4% -> 5% of each run, Pallas kernels for 0% -> 7%
where the time goes in v1:
time: 221 us; the launch traced here: 220 us
  waiting for transfers between devices  83.5 us (38%)
  starting transfers between devices  66.1 us (30%)
  Pallas kernels  50.4 us (23%)
  local copies, waits for them, and re-layouts  9.8 us (4%)
  other arithmetic  8.88 us (4%)
    ppermute x36, waiting for transfers between devices, permute(): return lax.ppermute(value, 'ctx', pairs)  83.5 us
    ppermute x36, starting transfers between devices, permute(): return lax.ppermute(value, 'ctx', pairs)  66.1 us
    pallas_call x5, Pallas kernels, call(): pl.pallas_call(kernel, grid_spec=grid_spec, out_shape=outs, interpret=INT...  50.4 us
    unnamed x76, local copies, waits for them, and re-layouts  6.54 us
  transfers between devices with their start and end apart: 36, of which 20 were waited for; matrix products, arithmetic and copies ran while one was open for 5% of the time, Pallas kernels for 7%

profile of v1, /device:TPU:16, one launch (start us, length us, event | category | flops | bytes accessed | tf_op | source)
XLA Modules:
  0.0 220.2 jit_solution(10653582729749821398)
XLA Ops:
  0.6 12.7 %shard_map.144 = (f32[528,128]{1,0:T(8,128)}, f32[528,128]{1,0:T(8,128)}, f32[528,128]{1,0:T(8,128)}, f32[528,128]{1,0:T(8,128)}, f32[2,512,128]{2,1,0:T(8,128)}...) custom-call(s32[1]{0:T(128)} %bitcast.x_ref.refs_0_, ...), custom_call_target="tpu_custom_call" | custom-call | tf_op jit(solution)/shard_map/pallas_call | solution.py:399
  13.4 1.6 collective-permute-start
  15.0 2.7 %collective-permute-start.1 = (f32[528,128]{1,0:T(8,128)}, f32[528,128]{1,0:T(8,128)S(1)}, u32[]{:S(2)}, u32[]{:S(2)}) collective-permute-start(f32[528,128]{1,0:T(8,128)} %get-tuple-element.42), channel_id=1, source_target_pairs={{0,16},{8,24},{16,0},{24,8},{32,48},{40,56},{48,32},{56,40},{64,80... | collective-permute-start | bytes 811016 | tf_op jit(solution)/shard_map/ppermute | solution.py:430
  18.2 2.2 collective-permute-start.6
  20.4 3.6 %collective-permute-start.5 = (f32[2,512,128]{2,1,0:T(8,128)}, f32[2,512,128]{2,1,0:T(8,128)S(1)}, u32[]{:S(2)}, u32[]{:S(2)}) collective-permute-start(f32[2,512,128]{2,1,0:T(8,128)} %get-tuple-element.47), channel_id=1, source_target_pairs={{0,8},{8,0},{16,24},{32,40},{40,32},{48,56},{64,72},{72,64},{80,88... | collective-permute-start | bytes 1572872 | tf_op jit(solution)/shard_map/ppermute | solution.py:430
  24.3 4.8 %shard_map.145.refs_3_ = f32[16,128,128]{2,1,0:T(8,128)} custom-call(bf16[128,2048]{1,0:T(8,128)(2,1)} %refs_1_.3, bf16[128,2048]{1,0:T(8,128)(2,1)} %key_ref.5, f32[4,128,8]{2,1,0:T(8,128)} %get-tuple-element.38.cols_ref.refs_3_, f32[4,8,128]{2,1,0:T(8,128)} %get-tuple-element.39.rows_ref.refs_4_, f32[4,4,128]{2,1,0:T(4,128)} %get-tuple-element.40.norm_ref.refs_5_, ...), custom_call_target="tpu_custom_call" | custom-call | tf_op jit(solution)/shard_map/pallas_call | solution.py:399
  29.1 2.0 collective-permute-done.1
  31.1 1.5 collective-permute-done.2
  32.8 2.0 collective-permute-start.3
  35.5 4.6 %collective-permute-done.6.refs_7_.refs_10_ = f32[2,512,128]{2,1,0:T(8,128)S(1)} collective-permute-done((f32[2,512,128]{2,1,0:T(8,128)}, f32[2,512,128]{2,1,0:T(8,128)S(1)}, u32[]{:S(2)}, u32[]{:S(2)}) %collective-permute-start.6) | collective-permute-done | bytes 524320 | tf_op jit(solution)/shard_map/ppermute | solution.py:430
  40.2 0.7 copy-done
  40.9 4.7 %collective-permute-start.8 = (f32[2,512,128]{2,1,0:T(8,128)S(1)}, f32[2,512,128]{2,1,0:T(8,128)S(1)}, u32[]{:S(2)}, u32[]{:S(2)}) collective-permute-start(f32[2,512,128]{2,1,0:T(8,128)S(1)} %bitcast.209), channel_id=1, source_target_pairs={{0,24},{8,16},{32,56},{40,48},{64,88},{72,80},{96,120},{104,112},{... | collective-permute-start | bytes 1572872 | tf_op jit(solution)/shard_map/ppermute | solution.py:430
  45.6 4.6 %collective-permute-done.5.refs_6_.refs_9_ = f32[2,512,128]{2,1,0:T(8,128)S(1)} collective-permute-done((f32[2,512,128]{2,1,0:T(8,128)}, f32[2,512,128]{2,1,0:T(8,128)S(1)}, u32[]{:S(2)}, u32[]{:S(2)}) %collective-permute-start.5) | collective-permute-done | bytes 524320 | tf_op jit(solution)/shard_map/ppermute | solution.py:430
  50.3 0.7 copy-done.1
  51.0 4.7 %collective-permute-start.7 = (f32[2,512,128]{2,1,0:T(8,128)S(1)}, f32[2,512,128]{2,1,0:T(8,128)S(1)}, u32[]{:S(2)}, u32[]{:S(2)}) collective-permute-start(f32[2,512,128]{2,1,0:T(8,128)S(1)} %bitcast.210), channel_id=1, source_target_pairs={{0,24},{8,16},{32,56},{40,48},{64,88},{72,80},{96,120},{104,112},{... | collective-permute-start | bytes 1572872 | tf_op jit(solution)/shard_map/ppermute | solution.py:430
  55.9 3.4 %collective-permute-start.4 = (f32[528,128]{1,0:T(8,128)S(1)}, f32[528,128]{1,0:T(8,128)S(1)}, u32[]{:S(2)}, u32[]{:S(2)}) collective-permute-start(f32[528,128]{1,0:T(8,128)S(1)} %pad_maximum_fusion.1), channel_id=1, source_target_pairs={{0,64},{8,72},{16,80},{24,88},{32,96},{40,104},{48,112},{56,120},{... | collective-permute-start | bytes 811016 | tf_op jit(solution)/shard_map/ppermute | solution.py:430
  59.5 0.9 add_select_fusion
  60.3 10.0 %collective-permute-done.4.refs_14_.refs_17_ = f32[528,128]{1,0:T(8,128)S(1)} collective-permute-done((f32[528,128]{1,0:T(8,128)S(1)}, f32[528,128]{1,0:T(8,128)S(1)}, u32[]{:S(2)}, u32[]{:S(2)}) %collective-permute-start.4) | collective-permute-done | bytes 270368 | tf_op jit(solution)/shard_map/ppermute | solution.py:430
  70.4 0.8 fusion.42
  71.2 5.3 %collective-permute-start.15 = (f32[528,128]{1,0:T(8,128)S(1)}, f32[528,128]{1,0:T(8,128)S(1)}, u32[]{:S(2)}, u32[]{:S(2)}) collective-permute-start(f32[528,128]{1,0:T(8,128)S(1)} %pad_maximum_fusion.2), channel_id=1, source_target_pairs={{0,224},{8,232},{16,240},{24,248},{32,192},{40,200},{48,208},{56,2... | collective-permute-start | bytes 811016 | tf_op jit(solution)/shard_map/ppermute | solution.py:430
  76.7 1.1 collective-permute-start.13
  77.8 3.7 %collective-permute-start.14 = (f32[528,128]{1,0:T(8,128)S(1)}, f32[528,128]{1,0:T(8,128)S(1)}, u32[]{:S(2)}, u32[]{:S(2)}) collective-permute-start(f32[528,128]{1,0:T(8,128)S(1)} %collective-permute-done.4.refs_14_.refs_17_), channel_id=1, source_target_pairs={{0,24},{8,16},{16,8},{24,0},{32,56},{40,48},{48,40},{56,32},{64,88... | collective-permute-start | bytes 811016 | tf_op jit(solution)/shard_map/ppermute | solution.py:430
  81.5 6.2 %collective-permute-done.15.refs_18_.refs_21_ = f32[528,128]{1,0:T(8,128)S(1)} collective-permute-done((f32[528,128]{1,0:T(8,128)S(1)}, f32[528,128]{1,0:T(8,128)S(1)}, u32[]{:S(2)}, u32[]{:S(2)}) %collective-permute-start.15) | collective-permute-done | bytes 270368 | tf_op jit(solution)/shard_map/ppermute | solution.py:430
  87.8 1.1 collective-permute-start.17
  88.8 2.0 collective-permute-done.13.refs_16_.refs_19_
  90.9 3.6 %collective-permute-start.18 = (f32[528,128]{1,0:T(8,128)S(1)}, f32[528,128]{1,0:T(8,128)S(1)}, u32[]{:S(2)}, u32[]{:S(2)}) collective-permute-start(f32[528,128]{1,0:T(8,128)S(1)} %collective-permute-done.15.refs_18_.refs_21_), channel_id=1, source_target_pairs={{0,24},{8,16},{16,8},{24,0},{32,56},{40,48},{48,40},{56,32},{64,88... | collective-permute-start | bytes 811016 | tf_op jit(solution)/shard_map/ppermute | solution.py:430
  95.2 2.4 %collective-permute-done.11.refs_12_.refs_15_ = f32[528,128]{1,0:T(8,128)S(1)} collective-permute-done((f32[528,128]{1,0:T(8,128)S(1)}, f32[528,128]{1,0:T(8,128)S(1)}, u32[]{:S(2)}, u32[]{:S(2)}) %collective-permute-start.11) | collective-permute-done | bytes 270368 | tf_op jit(solution)/shard_map/ppermute | solution.py:430
  97.6 5.8 %collective-permute-done.16.refs_19_.refs_22_ = f32[528,128]{1,0:T(8,128)S(1)} collective-permute-done((f32[528,128]{1,0:T(8,128)S(1)}, f32[528,128]{1,0:T(8,128)S(1)}, u32[]{:S(2)}, u32[]{:S(2)}) %collective-permute-start.16) | collective-permute-done | bytes 270368 | tf_op jit(solution)/shard_map/ppermute | solution.py:430
  103.4 3.2 %collective-permute-done.17.refs_20_.refs_23_ = f32[528,128]{1,0:T(8,128)S(1)} collective-permute-done((f32[528,128]{1,0:T(8,128)S(1)}, f32[528,128]{1,0:T(8,128)S(1)}, u32[]{:S(2)}, u32[]{:S(2)}) %collective-permute-start.17) | collective-permute-done | bytes 270368 | tf_op jit(solution)/shard_map/ppermute | solution.py:430
  106.6 0.7 copy-done.16
  107.5 13.7 %shard_map.146 = (f32[4,512,128]{2,1,0:T(8,128)}, f32[2,512,128]{2,1,0:T(8,128)}, f32[2,512,128]{2,1,0:T(8,128)}, f32[2,512,128]{2,1,0:T(8,128)}, f32[2,512,128]...) custom-call(s32[1]{0:T(128)} %bitcast.x_ref.refs_0_, ...), custom_call_target="tpu_custom_call" | custom-call | tf_op jit(solution)/shard_map/pallas_call | solution.py:399
  121.8 1.6 collective-permute-start.23
  123.3 3.1 %collective-permute-start.24 = (f32[520,128]{1,0:T(8,128)}, f32[520,128]{1,0:T(8,128)S(1)}, u32[]{:S(2)}, u32[]{:S(2)}) collective-permute-start(f32[520,128]{1,0:T(8,128)} %get-tuple-element.59), channel_id=1, source_target_pairs={{0,16},{8,24},{16,0},{24,8},{32,48},{40,56},{48,32},{56,40},{64,80... | collective-permute-start | bytes 798728 | tf_op jit(solution)/shard_map/ppermute | solution.py:430
  127.0 1.0 slice.301
  128.0 0.9 collective-permute-start.30
  128.9 13.1 %collective-permute-done.23 = f32[520,128]{1,0:T(8,128)S(1)} collective-permute-done((f32[520,128]{1,0:T(8,128)}, f32[520,128]{1,0:T(8,128)S(1)}, u32[]{:S(2)}, u32[]{:S(2)}) %collective-permute-start.23) | collective-permute-done | bytes 266272 | tf_op jit(solution)/shard_map/ppermute | solution.py:430
  142.0 1.3 collective-permute-start.19
  143.3 7.5 %collective-permute-done.24 = f32[520,128]{1,0:T(8,128)S(1)} collective-permute-done((f32[520,128]{1,0:T(8,128)}, f32[520,128]{1,0:T(8,128)S(1)}, u32[]{:S(2)}, u32[]{:S(2)}) %collective-permute-start.24) | collective-permute-done | bytes 266272 | tf_op jit(solution)/shard_map/ppermute | solution.py:430
  150.9 0.7 copy-done.25
  152.6 2.8 %collective-permute-start.28 = (f32[512,128]{1,0:T(8,128)S(1)}, f32[512,128]{1,0:T(8,128)S(1)}, u32[]{:S(2)}, u32[]{:S(2)}) collective-permute-start(f32[512,128]{1,0:T(8,128)S(1)} %fusion.19), channel_id=1, source_target_pairs={{0,24},{8,16},{16,8},{24,0},{32,56},{40,48},{48,40},{56,32},{64,88... | collective-permute-start | bytes 786440 | tf_op jit(solution)/shard_map/ppermute | solution.py:430
  155.4 1.0 collective-permute-done.30
  156.5 3.7 %collective-permute-start.31 = (f32[512,128]{1,0:T(8,128)S(1)}, f32[512,128]{1,0:T(8,128)S(1)}, u32[]{:S(2)}, u32[]{:S(2)}) collective-permute-start(f32[512,128]{1,0:T(8,128)S(1)} %fusion.16), channel_id=1, source_target_pairs={{0,24},{8,16},{16,8},{24,0},{32,56},{40,48},{48,40},{56,32},{64,88... | collective-permute-start | bytes 786440 | tf_op jit(solution)/shard_map/ppermute | solution.py:430
  160.2 2.1 collective-permute-done.26
  162.3 4.4 %collective-permute-done.28 = f32[512,128]{1,0:T(8,128)S(1)} collective-permute-done((f32[512,128]{1,0:T(8,128)S(1)}, f32[512,128]{1,0:T(8,128)S(1)}, u32[]{:S(2)}, u32[]{:S(2)}) %collective-permute-start.28) | collective-permute-done | bytes 262176 | tf_op jit(solution)/shard_map/ppermute | solution.py:430
  166.9 0.7 collective-permute-start.29
  167.6 1.0 copy-done.36
  168.6 1.3 collective-permute-start.20
  170.0 0.7 copy-done.5
  170.7 1.9 collective-permute-start.22
  172.6 4.0 %collective-permute-done.29 = f32[520,128]{1,0:T(8,128)S(1)} collective-permute-done((f32[520,128]{1,0:T(8,128)S(1)}, f32[520,128]{1,0:T(8,128)S(1)}, u32[]{:S(2)}, u32[]{:S(2)}) %collective-permute-start.29) | collective-permute-done | bytes 266272 | tf_op jit(solution)/shard_map/ppermute | solution.py:430
  176.8 0.8 pad_maximum_fusion.5
  177.6 3.3 %collective-permute-done.20.p1_ref = f32[2,512,128]{2,1,0:T(8,128)S(1)} collective-permute-done((f32[2,512,128]{2,1,0:T(8,128)S(1)}, f32[2,512,128]{2,1,0:T(8,128)S(1)}, u32[]{:S(2)}, u32[]{:S(2)}) %collective-permute-start.20) | collective-permute-done | bytes 524320 | tf_op jit(solution)/shard_map/ppermute | solution.py:430
  181.0 0.8 copy-done.6
  181.7 1.9 collective-permute-start.21
  183.7 1.4 select_bitcast_fusion
  185.1 10.4 %shard_map.147 = (bf16[128,2048]{1,0:T(8,128)(2,1)}, f32[16,128,128]{2,1,0:T(8,128)}, f32[16,128,128]{2,1,0:T(8,128)}) custom-call(s32[1]{0:T(128)} %bitcast.x_ref.refs_0_, bf16[128,2048]{1,0:T(8,128)(2,1)} %refs_1_.3, bf16[128,2048]{1,0:T(8,128)(2,1)} %key_ref.5, f32[4,128,8]{2,1,0:T(8,128)} %get-tuple-element.38.cols_ref.refs_3_, ...), custom_call_target="tpu_custom_call" | custom-call | tf_op jit(solution)/shard_map/pallas_call | solution.py:399
  195.5 1.1 fusion.9.a0_ref
  196.7 2.3 %collective-permute-start.33 = (f32[512,128]{1,0:T(8,128)S(1)}, f32[512,128]{1,0:T(8,128)S(1)}, u32[]{:S(2)}, u32[]{:S(2)}) collective-permute-start(f32[512,128]{1,0:T(8,128)S(1)} %fusion.9.a0_ref), channel_id=1, source_target_pairs={{0,8},{8,0},{16,24},{24,16},{32,40},{40,32},{48,56},{56,48},{64,72... | collective-permute-start | bytes 786440 | tf_op jit(solution)/shard_map/ppermute | solution.py:430
  199.0 2.8 %collective-permute-start.35 = (f32[512,128]{1,0:T(8,128)S(1)}, f32[512,128]{1,0:T(8,128)S(1)}, u32[]{:S(2)}, u32[]{:S(2)}) collective-permute-start(f32[512,128]{1,0:T(8,128)S(1)} %fusion.9.a0_ref), channel_id=1, source_target_pairs={{0,24},{8,16},{16,8},{24,0},{32,56},{40,48},{48,40},{56,32},{64,88... | collective-permute-start | bytes 786440 | tf_op jit(solution)/shard_map/ppermute | solution.py:430
  202.4 1.2 fusion.39
  204.0 3.0 %collective-permute-done.34.a2_ref = f32[512,128]{1,0:T(8,128)S(1)} collective-permute-done((f32[512,128]{1,0:T(8,128)S(1)}, f32[512,128]{1,0:T(8,128)S(1)}, u32[]{:S(2)}, u32[]{:S(2)}) %collective-permute-start.34) | collective-permute-done | bytes 262176 | tf_op jit(solution)/shard_map/ppermute | solution.py:430
  207.0 2.4 %collective-permute-done.35.a3_ref = f32[512,128]{1,0:T(8,128)S(1)} collective-permute-done((f32[512,128]{1,0:T(8,128)S(1)}, f32[512,128]{1,0:T(8,128)S(1)}, u32[]{:S(2)}, u32[]{:S(2)}) %collective-permute-start.35) | collective-permute-done | bytes 262176 | tf_op jit(solution)/shard_map/ppermute | solution.py:430
  210.1 8.8 %shard_map.148 = (bf16[128,2048]{1,0:T(8,128)(2,1)}, bf16[128,2048]{1,0:T(8,128)(2,1)}, f32[4,8,128]{2,1,0:T(8,128)}) custom-call(s32[1]{0:T(128)} %bitcast.x_ref.refs_0_, bf16[128,2048]{1,0:T(8,128)(2,1)} %key_ref.5, bf16[128,2048]{1,0:T(8,128)(2,1)} %value_ref.3, f32[4,128,8]{2,1,0:T(8,128)} %get-tuple-element.38.cols_ref.refs_3_, ...), custom_call_target="tpu_custom_call" | custom-call | tf_op jit(solution)/shard_map/pallas_call | solution.py:399
  218.9 1.3 slice.249
  (152 shorter events, 7.6 us)
Async XLA Ops:
  13.4 15.7 %collective-permute-start = (f32[528,128]{1,0:T(8,128)}, f32[528,128]{1,0:T(8,128)S(1)}, u32[]{:S(2)}, u32[]{:S(2)}) collective-permute-start(f32[528,128]{1,0:T(8,128)} %get-tuple-element.41), channel_id=1, source_target_pairs={{0,8},{8,0},{16,24},{24,16},{32,40},{40,32},{48,56},{56,48},{64,72... | collective-permute-start | bytes 811016 | tf_op jit(solution)/shard_map/ppermute | solution.py:430
  15.0 16.1 %collective-permute-start.1 = (f32[528,128]{1,0:T(8,128)}, f32[528,128]{1,0:T(8,128)S(1)}, u32[]{:S(2)}, u32[]{:S(2)}) collective-permute-start(f32[528,128]{1,0:T(8,128)} %get-tuple-element.42), channel_id=1, source_target_pairs={{0,16},{8,24},{16,0},{24,8},{32,48},{40,56},{48,32},{56,40},{64,80... | collective-permute-start | bytes 811016 | tf_op jit(solution)/shard_map/ppermute | solution.py:430
  17.7 14.9 %collective-permute-start.2 = (f32[528,128]{1,0:T(8,128)}, f32[528,128]{1,0:T(8,128)S(1)}, u32[]{:S(2)}, u32[]{:S(2)}) collective-permute-start(f32[528,128]{1,0:T(8,128)} %get-tuple-element.43), channel_id=1, source_target_pairs={{0,24},{8,16},{16,8},{24,0},{32,56},{40,48},{48,40},{56,32},{64,88... | collective-permute-start | bytes 811016 | tf_op jit(solution)/shard_map/ppermute | solution.py:430
  18.2 21.9 %collective-permute-start.6 = (f32[2,512,128]{2,1,0:T(8,128)}, f32[2,512,128]{2,1,0:T(8,128)S(1)}, u32[]{:S(2)}, u32[]{:S(2)}) collective-permute-start(f32[2,512,128]{2,1,0:T(8,128)} %get-tuple-element.48), channel_id=1, source_target_pairs={{0,8},{8,0},{16,24},{32,40},{40,32},{48,56},{64,72},{72,64},{80,88... | collective-permute-start | bytes 1572872 | tf_op jit(solution)/shard_map/ppermute | solution.py:430
  20.4 29.9 %collective-permute-start.5 = (f32[2,512,128]{2,1,0:T(8,128)}, f32[2,512,128]{2,1,0:T(8,128)S(1)}, u32[]{:S(2)}, u32[]{:S(2)}) collective-permute-start(f32[2,512,128]{2,1,0:T(8,128)} %get-tuple-element.47), channel_id=1, source_target_pairs={{0,8},{8,0},{16,24},{32,40},{40,32},{48,56},{64,72},{72,64},{80,88... | collective-permute-start | bytes 1572872 | tf_op jit(solution)/shard_map/ppermute | solution.py:430
  24.3 4.8 %copy-start.32 = (f32[4,8,128]{2,1,0:T(8,128)S(1)}, f32[4,8,128]{2,1,0:T(8,128)}, u32[]{:S(2)}) copy-start(f32[4,8,128]{2,1,0:T(8,128)} %get-tuple-element.39.rows_ref.refs_4_) | copy-start | bytes 49156
  24.3 8.4 %copy-start.31 = (f32[528,128]{1,0:T(8,128)S(1)}, f32[528,128]{1,0:T(8,128)}, u32[]{:S(2)}) copy-start(f32[528,128]{1,0:T(8,128)} %get-tuple-element.44) | copy-start | bytes 811012
  29.1 3.5 %copy-start.35 = (f32[16,128]{1,0:T(8,128)S(1)}, f32[16,128]{1,0:T(8,128)}, u32[]{:S(2)}) copy-start(f32[16,128]{1,0:T(8,128)} %get-tuple-element.45) | copy-start | bytes 24580
  32.8 7.3 %copy-start.21 = (f32[2,512,128]{2,1,0:T(8,128)S(1)}, f32[2,512,128]{2,1,0:T(8,128)}, u32[]{:S(2)}) copy-start(f32[2,512,128]{2,1,0:T(8,128)} %get-tuple-element.48) | copy-start | bytes 1572868
  32.8 22.9 %collective-permute-start.3 = (f32[528,128]{1,0:T(8,128)S(1)}, f32[528,128]{1,0:T(8,128)S(1)}, u32[]{:S(2)}, u32[]{:S(2)}) collective-permute-start(f32[528,128]{1,0:T(8,128)S(1)} %pad_maximum_fusion), channel_id=1, source_target_pairs={{0,32},{8,40},{16,48},{24,56},{32,0},{40,8},{48,16},{56,24},{64,96... | collective-permute-start | bytes 811016 | tf_op jit(solution)/shard_map/ppermute | solution.py:430
  40.1 10.1 %copy-start.20 = (f32[2,512,128]{2,1,0:T(8,128)S(1)}, f32[2,512,128]{2,1,0:T(8,128)}, u32[]{:S(2)}) copy-start(f32[2,512,128]{2,1,0:T(8,128)} %get-tuple-element.47) | copy-start | bytes 1572868
  40.9 36.8 %collective-permute-start.8 = (f32[2,512,128]{2,1,0:T(8,128)S(1)}, f32[2,512,128]{2,1,0:T(8,128)S(1)}, u32[]{:S(2)}, u32[]{:S(2)}) collective-permute-start(f32[2,512,128]{2,1,0:T(8,128)S(1)} %bitcast.209), channel_id=1, source_target_pairs={{0,24},{8,16},{32,56},{40,48},{64,88},{72,80},{96,120},{104,112},{... | collective-permute-start | bytes 1572872 | tf_op jit(solution)/shard_map/ppermute | solution.py:430
  51.0 30.5 %collective-permute-start.7 = (f32[2,512,128]{2,1,0:T(8,128)S(1)}, f32[2,512,128]{2,1,0:T(8,128)S(1)}, u32[]{:S(2)}, u32[]{:S(2)}) collective-permute-start(f32[2,512,128]{2,1,0:T(8,128)S(1)} %bitcast.210), channel_id=1, source_target_pairs={{0,24},{8,16},{32,56},{40,48},{64,88},{72,80},{96,120},{104,112},{... | collective-permute-start | bytes 1572872 | tf_op jit(solution)/shard_map/ppermute | solution.py:430
  55.7 20.8 %copy-start.2 = (f32[528,128]{1,0:T(8,128)}, f32[528,128]{1,0:T(8,128)S(1)}, u32[]{:S(2)}) copy-start(f32[528,128]{1,0:T(8,128)S(1)} %collective-permute-done.3.refs_10_.refs_13_) | copy-start | bytes 811012
  55.9 14.5 %collective-permute-start.4 = (f32[528,128]{1,0:T(8,128)S(1)}, f32[528,128]{1,0:T(8,128)S(1)}, u32[]{:S(2)}, u32[]{:S(2)}) collective-permute-start(f32[528,128]{1,0:T(8,128)S(1)} %pad_maximum_fusion.1), channel_id=1, source_target_pairs={{0,64},{8,72},{16,80},{24,88},{32,96},{40,104},{48,112},{56,120},{... | collective-permute-start | bytes 811016 | tf_op jit(solution)/shard_map/ppermute | solution.py:430
  59.3 17.3 %collective-permute-start.10 = (f32[528,128]{1,0:T(8,128)S(1)}, f32[528,128]{1,0:T(8,128)S(1)}, u32[]{:S(2)}, u32[]{:S(2)}) collective-permute-start(f32[528,128]{1,0:T(8,128)S(1)} %collective-permute-done.3.refs_10_.refs_13_), channel_id=1, source_target_pairs={{0,24},{8,16},{16,8},{24,0},{32,56},{40,48},{48,40},{56,32},{64,88... | collective-permute-start | bytes 811016 | tf_op jit(solution)/shard_map/ppermute | solution.py:430
  59.4 17.3 %collective-permute-start.9 = (f32[528,128]{1,0:T(8,128)S(1)}, f32[528,128]{1,0:T(8,128)S(1)}, u32[]{:S(2)}, u32[]{:S(2)}) collective-permute-start(f32[528,128]{1,0:T(8,128)S(1)} %collective-permute-done.3.refs_10_.refs_13_), channel_id=1, source_target_pairs={{0,8},{8,0},{16,24},{24,16},{32,40},{40,32},{48,56},{56,48},{64,72... | collective-permute-start | bytes 811016 | tf_op jit(solution)/shard_map/ppermute | solution.py:430
  70.4 7.4 %copy-start.3 = (f32[528,128]{1,0:T(8,128)}, f32[528,128]{1,0:T(8,128)S(1)}, u32[]{:S(2)}) copy-start(f32[528,128]{1,0:T(8,128)S(1)} %collective-permute-done.4.refs_14_.refs_17_) | copy-start | bytes 811012
  71.2 16.6 %collective-permute-start.15 = (f32[528,128]{1,0:T(8,128)S(1)}, f32[528,128]{1,0:T(8,128)S(1)}, u32[]{:S(2)}, u32[]{:S(2)}) collective-permute-start(f32[528,128]{1,0:T(8,128)S(1)} %pad_maximum_fusion.2), channel_id=1, source_target_pairs={{0,224},{8,232},{16,240},{24,248},{32,192},{40,200},{48,208},{56,2... | collective-permute-start | bytes 811016 | tf_op jit(solution)/shard_map/ppermute | solution.py:430
  76.5 1.2 copy-start.33
  76.5 30.9 %copy-start.9 = (f32[528,128]{1,0:T(8,128)}, f32[528,128]{1,0:T(8,128)S(1)}, u32[]{:S(2)}) copy-start(f32[528,128]{1,0:T(8,128)S(1)} %collective-permute-done.10.refs_13_.refs_16_) | copy-start | bytes 811012
  76.5 11.2 %collective-permute-start.12 = (f32[528,128]{1,0:T(8,128)S(1)}, f32[528,128]{1,0:T(8,128)S(1)}, u32[]{:S(2)}, u32[]{:S(2)}) collective-permute-start(f32[528,128]{1,0:T(8,128)S(1)} %collective-permute-done.4.refs_14_.refs_17_), channel_id=1, source_target_pairs={{0,8},{8,0},{16,24},{24,16},{32,40},{40,32},{48,56},{56,48},{64,72... | collective-permute-start | bytes 811016 | tf_op jit(solution)/shard_map/ppermute | solution.py:430
  76.6 30.8 %copy-start.10 = (f32[528,128]{1,0:T(8,128)}, f32[528,128]{1,0:T(8,128)S(1)}, u32[]{:S(2)}) copy-start(f32[528,128]{1,0:T(8,128)S(1)} %collective-permute-done.9.refs_11_.refs_14_) | copy-start | bytes 811012
  76.7 14.2 %collective-permute-start.13 = (f32[528,128]{1,0:T(8,128)S(1)}, f32[528,128]{1,0:T(8,128)S(1)}, u32[]{:S(2)}, u32[]{:S(2)}) collective-permute-start(f32[528,128]{1,0:T(8,128)S(1)} %collective-permute-done.4.refs_14_.refs_17_), channel_id=1, source_target_pairs={{0,16},{8,24},{16,0},{24,8},{32,48},{40,56},{48,32},{56,40},{64,80... | collective-permute-start | bytes 811016 | tf_op jit(solution)/shard_map/ppermute | solution.py:430
  77.8 29.7 %copy-start.7 = (f32[2,512,128]{2,1,0:T(8,128)}, f32[2,512,128]{2,1,0:T(8,128)S(1)}, u32[]{:S(2)}) copy-start(f32[2,512,128]{2,1,0:T(8,128)S(1)} %collective-permute-done.8.refs_9_.refs_12_) | copy-start | bytes 1572868
  77.8 17.4 %collective-permute-start.14 = (f32[528,128]{1,0:T(8,128)S(1)}, f32[528,128]{1,0:T(8,128)S(1)}, u32[]{:S(2)}, u32[]{:S(2)}) collective-permute-start(f32[528,128]{1,0:T(8,128)S(1)} %collective-permute-done.4.refs_14_.refs_17_), channel_id=1, source_target_pairs={{0,24},{8,16},{16,8},{24,0},{32,56},{40,48},{48,40},{56,32},{64,88... | collective-permute-start | bytes 811016 | tf_op jit(solution)/shard_map/ppermute | solution.py:430
  81.5 26.0 %copy-start.8 = (f32[2,512,128]{2,1,0:T(8,128)}, f32[2,512,128]{2,1,0:T(8,128)S(1)}, u32[]{:S(2)}) copy-start(f32[2,512,128]{2,1,0:T(8,128)S(1)} %collective-permute-done.7.refs_8_.refs_11_) | copy-start | bytes 1572868
  81.5 16.1 %collective-permute-start.11 = (f32[528,128]{1,0:T(8,128)S(1)}, f32[528,128]{1,0:T(8,128)S(1)}, u32[]{:S(2)}, u32[]{:S(2)}) collective-permute-start(f32[528,128]{1,0:T(8,128)S(1)} %collective-permute-done.10.refs_13_.refs_16_), channel_id=1, source_target_pairs={{0,8},{8,0},{16,24},{24,16},{32,40},{40,32},{48,56},{56,48},{64,72... | collective-permute-start | bytes 811016 | tf_op jit(solution)/shard_map/ppermute | solution.py:430
  87.7 19.7 %copy-start.4 = (f32[528,128]{1,0:T(8,128)}, f32[528,128]{1,0:T(8,128)S(1)}, u32[]{:S(2)}) copy-start(f32[528,128]{1,0:T(8,128)S(1)} %collective-permute-done.15.refs_18_.refs_21_) | copy-start | bytes 811012
  87.7 15.7 %collective-permute-start.16 = (f32[528,128]{1,0:T(8,128)S(1)}, f32[528,128]{1,0:T(8,128)S(1)}, u32[]{:S(2)}, u32[]{:S(2)}) collective-permute-start(f32[528,128]{1,0:T(8,128)S(1)} %collective-permute-done.15.refs_18_.refs_21_), channel_id=1, source_target_pairs={{0,8},{8,0},{16,24},{24,16},{32,40},{40,32},{48,56},{56,48},{64,72... | collective-permute-start | bytes 811016 | tf_op jit(solution)/shard_map/ppermute | solution.py:430
  87.7 19.7 %copy-start.11 = (f32[528,128]{1,0:T(8,128)}, f32[528,128]{1,0:T(8,128)S(1)}, u32[]{:S(2)}) copy-start(f32[528,128]{1,0:T(8,128)S(1)} %collective-permute-done.12.refs_15_.refs_18_) | copy-start | bytes 811012
  87.8 18.8 %collective-permute-start.17 = (f32[528,128]{1,0:T(8,128)S(1)}, f32[528,128]{1,0:T(8,128)S(1)}, u32[]{:S(2)}, u32[]{:S(2)}) collective-permute-start(f32[528,128]{1,0:T(8,128)S(1)} %collective-permute-done.15.refs_18_.refs_21_), channel_id=1, source_target_pairs={{0,16},{8,24},{16,0},{24,8},{32,48},{40,56},{48,32},{56,40},{64,80... | collective-permute-start | bytes 811016 | tf_op jit(solution)/shard_map/ppermute | solution.py:430
  90.9 16.6 %copy-start.12 = (f32[528,128]{1,0:T(8,128)}, f32[528,128]{1,0:T(8,128)S(1)}, u32[]{:S(2)}) copy-start(f32[528,128]{1,0:T(8,128)S(1)} %collective-permute-done.13.refs_16_.refs_19_) | copy-start | bytes 811012
  90.9 15.7 %collective-permute-start.18 = (f32[528,128]{1,0:T(8,128)S(1)}, f32[528,128]{1,0:T(8,128)S(1)}, u32[]{:S(2)}, u32[]{:S(2)}) collective-permute-start(f32[528,128]{1,0:T(8,128)S(1)} %collective-permute-done.15.refs_18_.refs_21_), channel_id=1, source_target_pairs={{0,24},{8,16},{16,8},{24,0},{32,56},{40,48},{48,40},{56,32},{64,88... | collective-permute-start | bytes 811016 | tf_op jit(solution)/shard_map/ppermute | solution.py:430
  95.2 12.3 %copy-start.13 = (f32[528,128]{1,0:T(8,128)}, f32[528,128]{1,0:T(8,128)S(1)}, u32[]{:S(2)}) copy-start(f32[528,128]{1,0:T(8,128)S(1)} %collective-permute-done.14.refs_17_.refs_20_) | copy-start | bytes 811012
  97.6 9.9 %copy-start.14 = (f32[528,128]{1,0:T(8,128)}, f32[528,128]{1,0:T(8,128)S(1)}, u32[]{:S(2)}) copy-start(f32[528,128]{1,0:T(8,128)S(1)} %collective-permute-done.11.refs_12_.refs_15_) | copy-start | bytes 811012
  103.4 3.2 %copy-start.15 = (f32[528,128]{1,0:T(8,128)}, f32[528,128]{1,0:T(8,128)S(1)}, u32[]{:S(2)}) copy-start(f32[528,128]{1,0:T(8,128)S(1)} %collective-permute-done.16.refs_19_.refs_22_) | copy-start | bytes 811012
  121.2 30.9 %collective-permute-start.27 = (f32[2,512,128]{2,1,0:T(8,128)}, f32[2,512,128]{2,1,0:T(8,128)S(1)}, u32[]{:S(2)}, u32[]{:S(2)}) collective-permute-start(f32[2,512,128]{2,1,0:T(8,128)} %get-tuple-element.62), channel_id=1, source_target_pairs={{0,8},{8,0},{16,24},{24,16},{32,40},{40,32},{48,56},{56,48},{64,72... | collective-permute-start | bytes 1572872 | tf_op jit(solution)/shard_map/ppermute | solution.py:430
  121.8 20.2 %collective-permute-start.23 = (f32[520,128]{1,0:T(8,128)}, f32[520,128]{1,0:T(8,128)S(1)}, u32[]{:S(2)}, u32[]{:S(2)}) collective-permute-start(f32[520,128]{1,0:T(8,128)} %get-tuple-element.58), channel_id=1, source_target_pairs={{0,8},{8,0},{16,24},{24,16},{32,40},{40,32},{48,56},{56,48},{64,72... | collective-permute-start | bytes 798728 | tf_op jit(solution)/shard_map/ppermute | solution.py:430
  123.3 27.4 %collective-permute-start.24 = (f32[520,128]{1,0:T(8,128)}, f32[520,128]{1,0:T(8,128)S(1)}, u32[]{:S(2)}, u32[]{:S(2)}) collective-permute-start(f32[520,128]{1,0:T(8,128)} %get-tuple-element.59), channel_id=1, source_target_pairs={{0,16},{8,24},{16,0},{24,8},{32,48},{40,56},{48,32},{56,40},{64,80... | collective-permute-start | bytes 798728 | tf_op jit(solution)/shard_map/ppermute | solution.py:430
  126.5 24.3 %collective-permute-start.25 = (f32[520,128]{1,0:T(8,128)}, f32[520,128]{1,0:T(8,128)S(1)}, u32[]{:S(2)}, u32[]{:S(2)}) collective-permute-start(f32[520,128]{1,0:T(8,128)} %get-tuple-element.60), channel_id=1, source_target_pairs={{0,24},{8,16},{16,8},{24,0},{32,56},{40,48},{48,40},{56,32},{64,88... | collective-permute-start | bytes 798728 | tf_op jit(solution)/shard_map/ppermute | solution.py:430
  127.0 23.8 %copy-start.27 = (f32[520,128]{1,0:T(8,128)S(1)}, f32[520,128]{1,0:T(8,128)}, u32[]{:S(2)}) copy-start(f32[520,128]{1,0:T(8,128)} %get-tuple-element.57) | copy-start | bytes 798724
  128.0 28.4 %collective-permute-start.30 = (f32[2,512,128]{2,1,0:T(8,128)}, f32[2,512,128]{2,1,0:T(8,128)S(1)}, u32[]{:S(2)}, u32[]{:S(2)}) collective-permute-start(f32[2,512,128]{2,1,0:T(8,128)} %get-tuple-element.64), channel_id=1, source_target_pairs={{0,8},{8,0},{16,24},{24,16},{32,40},{40,32},{48,56},{56,48},{64,72... | collective-permute-start | bytes 1572872 | tf_op jit(solution)/shard_map/ppermute | solution.py:430
  142.0 27.9 %collective-permute-start.19 = (f32[2,512,128]{2,1,0:T(8,128)}, f32[2,512,128]{2,1,0:T(8,128)S(1)}, u32[]{:S(2)}, u32[]{:S(2)}) collective-permute-start(f32[2,512,128]{2,1,0:T(8,128)} %get-tuple-element.54), channel_id=1, source_target_pairs={{16,8},{24,0},{48,40},{56,32},{80,72},{88,64},{112,104},{120,96},{... | collective-permute-start | bytes 1572872 | tf_op jit(solution)/shard_map/ppermute | solution.py:430
  151.7 4.7 %copy-start.23 = (f32[2,512,128]{2,1,0:T(8,128)S(1)}, f32[2,512,128]{2,1,0:T(8,128)}, u32[]{:S(2)}) copy-start(f32[2,512,128]{2,1,0:T(8,128)} %get-tuple-element.63) | copy-start | bytes 1572868
  151.7 10.6 %collective-permute-start.26 = (f32[520,128]{1,0:T(8,128)S(1)}, f32[520,128]{1,0:T(8,128)S(1)}, u32[]{:S(2)}, u32[]{:S(2)}) collective-permute-start(f32[520,128]{1,0:T(8,128)S(1)} %pad_maximum_fusion.3), channel_id=1, source_target_pairs={{0,224},{8,232},{16,240},{24,248},{32,192},{40,200},{48,208},{56,2... | collective-permute-start | bytes 798728 | tf_op jit(solution)/shard_map/ppermute | solution.py:430
  152.6 14.1 %collective-permute-start.28 = (f32[512,128]{1,0:T(8,128)S(1)}, f32[512,128]{1,0:T(8,128)S(1)}, u32[]{:S(2)}, u32[]{:S(2)}) collective-permute-start(f32[512,128]{1,0:T(8,128)S(1)} %fusion.19), channel_id=1, source_target_pairs={{0,24},{8,16},{16,8},{24,0},{32,56},{40,48},{48,40},{56,32},{64,88... | collective-permute-start | bytes 786440 | tf_op jit(solution)/shard_map/ppermute | solution.py:430
  156.5 11.1 %copy-start.18 = (f32[4,512,128]{2,1,0:T(8,128)S(1)}, f32[4,512,128]{2,1,0:T(8,128)}, u32[]{:S(2)}) copy-start(f32[4,512,128]{2,1,0:T(8,128)} %get-tuple-element.56) | copy-start | bytes 3145732
  156.5 16.1 %collective-permute-start.31 = (f32[512,128]{1,0:T(8,128)S(1)}, f32[512,128]{1,0:T(8,128)S(1)}, u32[]{:S(2)}, u32[]{:S(2)}) collective-permute-start(f32[512,128]{1,0:T(8,128)S(1)} %fusion.16), channel_id=1, source_target_pairs={{0,24},{8,16},{16,8},{24,0},{32,56},{40,48},{48,40},{56,32},{64,88... | collective-permute-start | bytes 786440 | tf_op jit(solution)/shard_map/ppermute | solution.py:430
  166.9 9.7 %collective-permute-start.29 = (f32[520,128]{1,0:T(8,128)S(1)}, f32[520,128]{1,0:T(8,128)S(1)}, u32[]{:S(2)}, u32[]{:S(2)}) collective-permute-start(f32[520,128]{1,0:T(8,128)S(1)} %pad_maximum_fusion.4), channel_id=1, source_target_pairs={{0,64},{8,72},{16,80},{24,88},{32,96},{40,104},{48,112},{56,120},{... | collective-permute-start | bytes 798728 | tf_op jit(solution)/shard_map/ppermute | solution.py:430
  167.6 1.0 copy-start.36
  168.6 12.3 %collective-permute-start.20 = (f32[2,512,128]{2,1,0:T(8,128)S(1)}, f32[2,512,128]{2,1,0:T(8,128)S(1)}, u32[]{:S(2)}, u32[]{:S(2)}) collective-permute-start(f32[2,512,128]{2,1,0:T(8,128)S(1)} %copy-done.36), channel_id=1, source_target_pairs={{16,8},{24,0},{48,40},{56,32},{80,72},{88,64},{112,104},{120,96},{... | collective-permute-start | bytes 1572872 | tf_op jit(solution)/shard_map/ppermute | solution.py:430
  170.7 32.9 %collective-permute-start.22 = (f32[2,512,128]{2,1,0:T(8,128)S(1)}, f32[2,512,128]{2,1,0:T(8,128)S(1)}, u32[]{:S(2)}, u32[]{:S(2)}) collective-permute-start(f32[2,512,128]{2,1,0:T(8,128)S(1)} %bitcast.208), channel_id=1, source_target_pairs={{0,8},{8,0},{24,16},{32,40},{40,32},{56,48},{64,72},{72,64},{88,80... | collective-permute-start | bytes 1572872 | tf_op jit(solution)/shard_map/ppermute | solution.py:430
  177.5 18.0 %collective-permute-start.32 = (f32[520,128]{1,0:T(8,128)}, f32[520,128]{1,0:T(8,128)}, u32[]{:S(2)}, u32[]{:S(2)}) collective-permute-start(f32[520,128]{1,0:T(8,128)} %pad_maximum_fusion.5), channel_id=1, source_target_pairs={{0,32},{8,40},{16,48},{24,56},{32,0},{40,8},{48,16},{56,24},{64,96... | collective-permute-start | bytes 798728 | tf_op jit(solution)/shard_map/ppermute | solution.py:430
  181.7 21.9 %collective-permute-start.21 = (f32[2,512,128]{2,1,0:T(8,128)S(1)}, f32[2,512,128]{2,1,0:T(8,128)S(1)}, u32[]{:S(2)}, u32[]{:S(2)}) collective-permute-start(f32[2,512,128]{2,1,0:T(8,128)S(1)} %bitcast.211), channel_id=1, source_target_pairs={{0,8},{8,0},{24,16},{32,40},{40,32},{56,48},{64,72},{72,64},{88,80... | collective-permute-start | bytes 1572872 | tf_op jit(solution)/shard_map/ppermute | solution.py:430
  183.6 1.5 copy-start.34
  196.7 12.7 %copy-start.19 = (f32[512,128]{1,0:T(8,128)}, f32[512,128]{1,0:T(8,128)S(1)}, u32[]{:S(2)}) copy-start(f32[512,128]{1,0:T(8,128)S(1)} %fusion.9.a0_ref) | copy-start | bytes 786436
  196.7 7.3 %collective-permute-start.33 = (f32[512,128]{1,0:T(8,128)S(1)}, f32[512,128]{1,0:T(8,128)S(1)}, u32[]{:S(2)}, u32[]{:S(2)}) collective-permute-start(f32[512,128]{1,0:T(8,128)S(1)} %fusion.9.a0_ref), channel_id=1, source_target_pairs={{0,8},{8,0},{16,24},{24,16},{32,40},{40,32},{48,56},{56,48},{64,72... | collective-permute-start | bytes 786440 | tf_op jit(solution)/shard_map/ppermute | solution.py:430
  199.0 8.0 %collective-permute-start.34 = (f32[512,128]{1,0:T(8,128)S(1)}, f32[512,128]{1,0:T(8,128)S(1)}, u32[]{:S(2)}, u32[]{:S(2)}) collective-permute-start(f32[512,128]{1,0:T(8,128)S(1)} %fusion.9.a0_ref), channel_id=1, source_target_pairs={{0,16},{8,24},{16,0},{24,8},{32,48},{40,56},{48,32},{56,40},{64,80... | collective-permute-start | bytes 786440 | tf_op jit(solution)/shard_map/ppermute | solution.py:430
  199.0 10.4 %collective-permute-start.35 = (f32[512,128]{1,0:T(8,128)S(1)}, f32[512,128]{1,0:T(8,128)S(1)}, u32[]{:S(2)}, u32[]{:S(2)}) collective-permute-start(f32[512,128]{1,0:T(8,128)S(1)} %fusion.9.a0_ref), channel_id=1, source_target_pairs={{0,24},{8,16},{16,8},{24,0},{32,56},{40,48},{48,40},{56,32},{64,88... | collective-permute-start | bytes 786440 | tf_op jit(solution)/shard_map/ppermute | solution.py:430
  203.6 5.8 %copy-start.22 = (f32[2,512,128]{2,1,0:T(8,128)}, f32[2,512,128]{2,1,0:T(8,128)S(1)}, u32[]{:S(2)}) copy-start(f32[2,512,128]{2,1,0:T(8,128)S(1)} %collective-permute-done.22.n1_ref) | copy-start | bytes 1572868
  203.6 5.8 %copy-start.24 = (f32[2,512,128]{2,1,0:T(8,128)}, f32[2,512,128]{2,1,0:T(8,128)S(1)}, u32[]{:S(2)}) copy-start(f32[2,512,128]{2,1,0:T(8,128)S(1)} %collective-permute-done.21.n0_ref) | copy-start | bytes 1572868
  204.0 5.4 %copy-start.28 = (f32[512,128]{1,0:T(8,128)}, f32[512,128]{1,0:T(8,128)S(1)}, u32[]{:S(2)}) copy-start(f32[512,128]{1,0:T(8,128)S(1)} %collective-permute-done.33.a1_ref) | copy-start | bytes 786436
  207.0 2.4 %copy-start.29 = (f32[512,128]{1,0:T(8,128)}, f32[512,128]{1,0:T(8,128)S(1)}, u32[]{:S(2)}) copy-start(f32[512,128]{1,0:T(8,128)S(1)} %collective-permute-done.34.a2_ref) | copy-start | bytes 786436
  (9 other events, 7.3 us)

commit v2 on v1

--- a/solution.py
+++ b/solution.py
@@ -15,6 +15,7 @@
 LEVELS = 5
 INTERPRET = False
 
+
 NN = ((1,), (0,))
 NT = ((1,), (1,))
 TN = ((0,), (0,))
@@ -41,7 +42,7 @@
 
 def dot_split(a, b, dims=NN):
     ca, cb = dims[0][0], dims[1][0]
-    return dot(cat([a[0], a[1]], ca), cat([b[0], b[0]], cb), dims) + dot(a[0], b[1], dims)
+    return dot(cat([a[0], a[1], a[0]], ca), cat([b[0], b[0], b[1]], cb), dims)
 
 
 def dot_full(a, b, dims=NN):
@@ -180,7 +181,7 @@
 
 
 def place_pieces(x, pieces, scratch_ref):
-    for level in range(3):
+    for level in range(len(pieces) // 4):
         for m in range(4):
             scratch_ref[level, x ^ m] = pieces[4 * level + m][...]
 
@@ -203,80 +204,129 @@
     return cat(parts, 0)
 
 
-def cross_kernel(*refs):
-    x_ref, query_ref, out_ref, intra_ref, weight_ref, gain_ref = refs[:6]
-    near_refs, pair_refs, pieces = refs[6:8], refs[8:10], refs[10:22]
-    g1_ref, g2_refs = refs[22], refs[23:25]
-    g34_refs, g5_refs = refs[25:29], refs[29:33]
-    dm_ref, level_ref = refs[33:35]
-    scratch_ref, gather_ref, gain_sum_ref = refs[35:38]
+def read_buckets(qb, buckets):
+    pairs = [split(b) for b in buckets]
+    return dot(cat([qb, qb], 1), cat([cat([p[0] for p in pairs], 1), cat([p[1] for p in pairs], 1)], 0), NN)
+
+
+def bucket_grads(qb, weighted):
+    pairs = [split(w) for w in weighted]
+    return dot(cat([qb, qb], 0), cat([cat([p[0] for p in pairs], 1), cat([p[1] for p in pairs], 1)], 0), TN)
+
+
+def scaled_columns(weights, rq_col, j, levels):
+    scaled = weights * rq_col
+    return [jnp.broadcast_to(scaled[:, l * GROUP + j : l * GROUP + j + 1], (N, N)) for l in levels]
+
+
+def early_kernel(*refs):
+    x_ref, query_ref, intra_ref, weight_ref = refs[:4]
+    near_refs, pair_refs, pieces = refs[4:6], refs[6:8], refs[8:12]
+    cross_ref, mix_ref, scratch_ref = refs[12:15]
+    x = x_ref[0]
+    group = range(GROUP)
+    place_pieces(x, pieces, scratch_ref)
+    weights = weight_ref[0].T
+    qb = [query_ref[:, j * N : (j + 1) * N] for j in group]
+    crosses = [
+        read_buckets(qb[j], [bucket_of(x, j, level, near_refs, pair_refs, scratch_ref) for level in range(3)])
+        for j in group
+    ]
+    for j in group:
+        cross_ref[j] = crosses[j]
+        columns = scaled_columns(weights, inv_norm_col(qb[j].astype(F32)), j, (1, 2, 3))
+        mixture = weights[:, j : j + 1] * intra_ref[j]
+        for level in range(3):
+            mixture = mixture + columns[level] * crosses[j][:, level * N : (level + 1) * N]
+        mix_ref[j] = mixture
+
+
+def norm_kernel(*refs):
+    x_ref, query_ref, out_ref, mix_ref, weight_ref, gain_ref = refs[:6]
+    pieces = refs[6:14]
+    cross_ref, dm_ref, g5_refs, g4_refs, g2_refs = refs[14], refs[15], refs[16:20], refs[20:22], refs[22:24]
+    scratch_ref, gather_ref, gain_sum_ref = refs[24:27]
     step = pl.program_id(0)
     x = x_ref[0]
     group = range(GROUP)
     place_pieces(x, pieces, scratch_ref)
     gain = gain_ref[...]
-    lane = lax.broadcasted_iota(jnp.int32, (N, 8 * GROUP), 1)
     gain_sum = jnp.zeros((8, N), F32)
     weights = weight_ref[0].T
-    levels = jnp.zeros((N, 8 * GROUP), F32)
     qb = [query_ref[:, j * N : (j + 1) * N] for j in group]
-    crosses = []
-    for j in group:
-        pairs = [split(bucket_of(x, j, level, near_refs, pair_refs, scratch_ref)) for level in range(LEVELS)]
-        right = cat([cat([p[0] for p in pairs], 1), cat([p[1] for p in pairs], 1)], 0)
-        crosses.append(dot(cat([qb[j], qb[j]], 1), right, NN))
-    lefts = []
-    for j in group:
+    crosses = [
+        read_buckets(qb[j], [bucket_of(x, j, level, (), (), scratch_ref) for level in (2, 3)]) for j in group
+    ]
+    weighted = []
+    for j in group:
+        cross_ref[j] = crosses[j]
         go = out_ref[:, j * N : (j + 1) * N].astype(F32)
-        rq_col = inv_norm_col(qb[j].astype(F32))
-        scaled_weights = weights * jnp.where(lane < GROUP, 1.0, rq_col)
-        columns = [
-            jnp.broadcast_to(scaled_weights[:, l * GROUP + j : l * GROUP + j + 1], (N, N)) for l in range(LEVELS + 1)
-        ]
-        intra = intra_ref[j]
-        mixture = columns[0] * intra
-        for level in range(LEVELS):
-            mixture = mixture + columns[level + 1] * crosses[j][:, level * N : (level + 1) * N]
+        columns = scaled_columns(weights, inv_norm_col(qb[j].astype(F32)), j, (4, 5, 2))
+        mixture = mix_ref[j] + columns[0] * crosses[j][:, :N] + columns[1] * crosses[j][:, N:]
         inverse_rms = lax.rsqrt(jnp.mean(mixture * mixture, axis=1, keepdims=True) + EPS)
         scaled = mixture * inverse_rms
         gain_sum = gain_sum + (go * scaled).reshape(N // 8, 8, N).sum(axis=0)
         dn = go * gain
         dm = inverse_rms * (dn - scaled * jnp.mean(dn * scaled, axis=1, keepdims=True))
         dm_ref[j] = dm
-        levels = jnp.where(lane == j, jnp.sum(dm * intra, axis=1, keepdims=True), levels)
-        pairs = []
+        weighted.append([dm * c for c in columns])
+    for j in group:
+        grads = bucket_grads(qb[j], weighted[j])
+        rows = slice((j >> 1) * HALF, (j >> 1) * HALF + HALF)
+        for half in range(2):
+            for level in range(3):
+                gather_ref[level, 2 * (j & 1) + half, rows, :] = grads[
+                    half * HALF : (half + 1) * HALF, level * N : (level + 1) * N
+                ]
+    base = pl.multiple_of(step * N, N)
+    for m in range(4):
+        g4_refs[m in (1, 2)][m >> 1] = gather_ref[0, x ^ m]
+        g5_refs[m][pl.ds(base, N), :] = gather_ref[1, x ^ m]
+        g2_refs[m >> 1][m & 1] = gather_ref[2, x ^ m]
+
+    @pl.when(step == 0)
+    def _():
+        gain_sum_ref[...] = jnp.zeros((8, N), F32)
+
+    gain_sum_ref[...] += gain_sum
+
+    @pl.when(step == pl.num_programs(0) - 1)
+    def _():
+        for m in range(4):
+            g5_refs[m][4 * N : 4 * N + 8, :] = gain_sum_ref[...]
+
+
+def late_kernel(*refs):
+    x_ref, query_ref, intra_ref, weight_ref, early_ref, last_ref, dm_ref = refs[:7]
+    g1_ref, g3_refs, level_ref, gather_ref = refs[7], refs[8:10], refs[10], refs[11]
+    x = x_ref[0]
+    group = range(GROUP)
+    lane = lax.broadcasted_iota(jnp.int32, (N, 8 * GROUP), 1)
+    weights = weight_ref[0].T
+    levels = jnp.zeros((N, 8 * GROUP), F32)
+    qb = [query_ref[:, j * N : (j + 1) * N] for j in group]
+    weighted = []
+    for j in group:
+        dm = dm_ref[j]
+        rq_col = inv_norm_col(qb[j].astype(F32))
+        columns = scaled_columns(weights, rq_col, j, (1, 3))
+        weighted.append([dm * c for c in columns])
+        levels = jnp.where(lane == j, jnp.sum(dm * intra_ref[j], axis=1, keepdims=True), levels)
         for level in range(LEVELS):
-            along = jnp.sum(dm * crosses[j][:, level * N : (level + 1) * N], axis=1, keepdims=True) * rq_col
+            ref, at = (early_ref, level) if level < 3 else (last_ref, level - 3)
+            along = jnp.sum(dm * ref[j, :, at * N : (at + 1) * N], axis=1, keepdims=True) * rq_col
             levels = jnp.where(lane == (level + 1) * GROUP + j, along, levels)
-            pairs.append(split(dm * columns[level + 1]))
-        lefts.append(cat([cat([p[0] for p in pairs], 1), cat([p[1] for p in pairs], 1)], 0))
     level_ref[0] = levels.T
     for j in group:
-        grads = dot(cat([qb[j], qb[j]], 0), lefts[j], TN)
+        grads = bucket_grads(qb[j], weighted[j])
         rows = slice((j >> 1) * HALF, (j >> 1) * HALF + HALF)
         for half in range(2):
             quarter = 2 * (j & 1) + half
             part = grads[half * HALF : (half + 1) * HALF]
             g1_ref[x ^ quarter, rows, :] = part[:, 0:N]
-            for level in range(4):
-                gather_ref[level, quarter, rows, :] = part[:, (1 + level) * N : (2 + level) * N]
-    base = pl.multiple_of(step * N, N)
+            gather_ref[quarter, rows, :] = part[:, N : 2 * N]
     for m in range(4):
-        g2_refs[m >> 1][m & 1] = gather_ref[0, x ^ m]
-        for level in range(2):
-            g34_refs[2 * level + (m in (1, 2))][m >> 1] = gather_ref[1 + level, x ^ m]
-        g5_refs[m][pl.ds(base, N), :] = gather_ref[3, x ^ m]
-
-    @pl.when(step == 0)
-    def _():
-        gain_sum_ref[...] = jnp.zeros((8, N), F32)
-
-    gain_sum_ref[...] += gain_sum
-
-    @pl.when(step == pl.num_programs(0) - 1)
-    def _():
-        for m in range(4):
-            g5_refs[m][4 * N : 4 * N + 8, :] = gain_sum_ref[...]
+        g3_refs[m in (1, 2)][m >> 1] = gather_ref[x ^ m]
 
 
 def query_kernel(*refs):
@@ -512,24 +562,35 @@
     weights = jnp.pad(level_weight.transpose(2, 1, 0) * growth, ((0, 2), (0, 0), (0, 0)))
     weights = weights.reshape(8, 4, GROUP, N).transpose(1, 0, 2, 3).reshape(4, 8 * GROUP, N)
 
+    crosses, mixed = call(
+        early_kernel, (xs,), (query, intra, weights, *nears, *pairs, *pieces[:4]),
+        [TOKENS, SQUARE, WEIGHTS] + [PAIRS] * 4 + [PIECE] * 4,
+        [shape(heads, N, 3 * N), square], [spec((GROUP, N, 3 * N), lambda i: (i, 0, 0)), SQUARE],
+        scratch=[pltpu.VMEM((1, 4, N, N), F32)],
+    )
+    last_crosses, grad_mixture, *outs = call(
+        norm_kernel, (xs,), (query, grad_out, mixed, weights, norm_gain.reshape(1, N), *pieces[4:]),
+        [TOKENS, TOKENS, SQUARE, WEIGHTS, spec((1, N), lambda i: (0, 0))] + [PIECE] * 8,
+        [shape(heads, N, 2 * N), square] + [shape(4 * N + 8, N)] * 4 + [shape(2, 4 * N, N)] * 4,
+        [spec((GROUP, N, 2 * N), lambda i: (i, 0, 0)), SQUARE] + [spec((4 * N + 8, N), lambda i: (0, 0))] * 4
+        + [PAIRS] * 4,
+        scratch=[pltpu.VMEM((2, 4, N, N), F32), pltpu.VMEM((3, 4, N, N), F32), pltpu.VMEM((8, N), F32)],
+    )
+    grads5, grads4, grad_pairs = outs[:4], outs[4:6], outs[6:]
     outs = call(
-        cross_kernel, (xs,),
-        (query, grad_out, intra, weights, norm_gain.reshape(1, N), *nears, *pairs, *pieces),
-        [TOKENS, TOKENS, SQUARE, WEIGHTS, spec((1, N), lambda i: (0, 0))] + [PAIRS] * 4 + [PIECE] * 12,
-        [shape(4, 4 * N, N)] + [shape(2, 4 * N, N)] * 6 + [shape(4 * N + 8, N)] * 4 + [square, shape(4, 8 * GROUP, N)],
-        [SLOTS] + [PAIRS] * 6
-        + [spec((4 * N + 8, N), lambda i: (0, 0))] * 4 + [SQUARE, WEIGHTS],
-        scratch=[pltpu.VMEM((3, 4, N, N), F32), pltpu.VMEM((4, 4, N, N), F32), pltpu.VMEM((8, N), F32)],
-    )
-    grad_near, grad_pairs = outs[0], outs[1:3]
-    grads34, grads5 = outs[3:7], outs[7:11]
-    grad_mixture, grad_level_rows = outs[11:]
+        late_kernel, (xs,), (query, intra, weights, crosses, last_crosses, grad_mixture),
+        [TOKENS, SQUARE, WEIGHTS, spec((GROUP, N, 3 * N), lambda i: (i, 0, 0))]
+        + [spec((GROUP, N, 2 * N), lambda i: (i, 0, 0)), SQUARE],
+        [shape(4, 4 * N, N)] + [shape(2, 4 * N, N)] * 2 + [shape(4, 8 * GROUP, N)],
+        [SLOTS] + [PAIRS] * 2 + [WEIGHTS],
+        scratch=[pltpu.VMEM((4, N, N), F32)],
+    )
+    grad_near, grads3, grad_level_rows = outs[0], outs[1:3], outs[3]
 
     top = grads5[0] + sum(permute(grads5[m], m) for m in range(1, 4))
     pair_backs = [permute(g, 3, only=(2, 3)) for g in grad_pairs]
     middle = []
-    for level in range(2):
-        kept, sent = grads34[2 * level : 2 * level + 2]
+    for kept, sent in (grads3, grads4):
         first = permute(sent, 1)
         second = permute(kept[1] + first[1], 3)
         middle.append(kept[0] + first[0] + second)

time: 221 us -> 217 us (0.982)
  waiting for transfers between devices: 83.5 us -> 71.9 us
  Pallas kernels: 50.4 us -> 61.1 us
  local copies, waits for them, and re-layouts: 9.8 us -> 4.65 us
  other arithmetic: 8.88 us -> 12.9 us
    ppermute x36, waiting for transfers between devices: 83.5 us -> 71.9 us  [permute(): return lax.ppermute(value, 'ctx', pairs)]
    pallas_call x5 -> x7, Pallas kernels: 50.4 us -> 61.1 us  [call(): pl.pallas_call(kernel, grid_spec=grid_spec, out_shape=outs, interpret=INT...]
    unnamed x76 -> x72, local copies, waits for them, and re-layouts: 6.54 us -> 1.43 us
  transfers between devices with their start and end apart: 36 -> 36, of which waited for: 20 -> 20; matrix products, arithmetic and copies ran while one was open for 5% -> 7% of each run, Pallas kernels for 7% -> 14%
where the time goes in v2:
time: 217 us; the launch traced here: 216 us
  waiting for transfers between devices  71.9 us (33%)
  starting transfers between devices  64.2 us (30%)
  Pallas kernels  61.1 us (28%)
  other arithmetic  12.9 us (6%)
  local copies, waits for them, and re-layouts  4.65 us (2%)
    ppermute x36, waiting for transfers between devices, permute(): return lax.ppermute(value, 'ctx', pairs)  71.9 us
    ppermute x36, starting transfers between devices, permute(): return lax.ppermute(value, 'ctx', pairs)  64.2 us
    pallas_call x7, Pallas kernels, call(): pl.pallas_call(kernel, grid_spec=grid_spec, out_shape=outs, interpret=INT...  61.1 us
  transfers between devices with their start and end apart: 36, of which 20 were waited for; matrix products, arithmetic and copies ran while one was open for 7% of the time, Pallas kernels for 14%

profile of v2, /device:TPU:16, one launch (start us, length us, event | category | flops | bytes accessed | tf_op | source)
XLA Modules:
  0.0 216.1 jit_solution(2343422094087687553)
XLA Ops:
  0.6 12.6 %shard_map.144 = (f32[528,128]{1,0:T(8,128)}, f32[528,128]{1,0:T(8,128)}, f32[528,128]{1,0:T(8,128)}, f32[528,128]{1,0:T(8,128)}, f32[2,512,128]{2,1,0:T(8,128)}...) custom-call(s32[1]{0:T(128)} %bitcast.x_ref.refs_0_, ...), custom_call_target="tpu_custom_call" | custom-call | tf_op jit(solution)/shard_map/pallas_call | solution.py:449
  13.3 1.6 collective-permute-start
  14.9 2.7 %collective-permute-start.1 = (f32[528,128]{1,0:T(8,128)}, f32[528,128]{1,0:T(8,128)S(1)}, u32[]{:S(2)}, u32[]{:S(2)}) collective-permute-start(f32[528,128]{1,0:T(8,128)} %get-tuple-element.45), channel_id=1, source_target_pairs={{0,16},{8,24},{16,0},{24,8},{32,48},{40,56},{48,32},{56,40},{64,80... | collective-permute-start | bytes 811016 | tf_op jit(solution)/shard_map/ppermute | solution.py:480
  18.1 2.2 %collective-permute-start.6 = (f32[2,512,128]{2,1,0:T(8,128)}, f32[2,512,128]{2,1,0:T(8,128)S(1)}, u32[]{:S(2)}, u32[]{:S(2)}) collective-permute-start(f32[2,512,128]{2,1,0:T(8,128)} %get-tuple-element.51), channel_id=1, source_target_pairs={{0,8},{8,0},{16,24},{32,40},{40,32},{48,56},{64,72},{72,64},{80,88... | collective-permute-start | bytes 1572872 | tf_op jit(solution)/shard_map/ppermute | solution.py:480
  20.3 3.6 %collective-permute-start.5 = (f32[2,512,128]{2,1,0:T(8,128)}, f32[2,512,128]{2,1,0:T(8,128)S(1)}, u32[]{:S(2)}, u32[]{:S(2)}) collective-permute-start(f32[2,512,128]{2,1,0:T(8,128)} %get-tuple-element.50), channel_id=1, source_target_pairs={{0,8},{8,0},{16,24},{32,40},{40,32},{48,56},{64,72},{72,64},{80,88... | collective-permute-start | bytes 1572872 | tf_op jit(solution)/shard_map/ppermute | solution.py:480
  24.7 4.8 %shard_map.145.refs_2_ = f32[16,128,128]{2,1,0:T(8,128)} custom-call(bf16[128,2048]{1,0:T(8,128)(2,1)} %refs_1_.7, bf16[128,2048]{1,0:T(8,128)(2,1)} %key_ref.5, f32[4,128,8]{2,1,0:T(8,128)} %get-tuple-element.41.cols_ref.refs_3_, f32[4,8,128]{2,1,0:T(8,128)} %get-tuple-element.42.rows_ref.refs_4_, f32[4,4,128]{2,1,0:T(4,128)} %get-tuple-element.43.norm_ref.refs_5_, ...), custom_call_target="tpu_custom_call" | custom-call | tf_op jit(solution)/shard_map/pallas_call | solution.py:449
  29.5 1.4 collective-permute-done.1
  31.0 1.5 collective-permute-done.2
  32.7 2.0 collective-permute-start.3
  36.6 3.4 %collective-permute-done.6.refs_5_.refs_10_ = f32[2,512,128]{2,1,0:T(8,128)S(1)} collective-permute-done((f32[2,512,128]{2,1,0:T(8,128)}, f32[2,512,128]{2,1,0:T(8,128)S(1)}, u32[]{:S(2)}, u32[]{:S(2)}) %collective-permute-start.6) | collective-permute-done | bytes 524320 | tf_op jit(solution)/shard_map/ppermute | solution.py:480
  40.1 4.7 %collective-permute-start.8 = (f32[2,512,128]{2,1,0:T(8,128)S(1)}, f32[2,512,128]{2,1,0:T(8,128)S(1)}, u32[]{:S(2)}, u32[]{:S(2)}) collective-permute-start(f32[2,512,128]{2,1,0:T(8,128)S(1)} %bitcast.211), channel_id=1, source_target_pairs={{0,24},{8,16},{32,56},{40,48},{64,88},{72,80},{96,120},{104,112},{... | collective-permute-start | bytes 1572872 | tf_op jit(solution)/shard_map/ppermute | solution.py:480
  44.8 5.3 %collective-permute-done.5.refs_4_.refs_9_ = f32[2,512,128]{2,1,0:T(8,128)S(1)} collective-permute-done((f32[2,512,128]{2,1,0:T(8,128)}, f32[2,512,128]{2,1,0:T(8,128)S(1)}, u32[]{:S(2)}, u32[]{:S(2)}) %collective-permute-start.5) | collective-permute-done | bytes 524320 | tf_op jit(solution)/shard_map/ppermute | solution.py:480
  50.2 4.7 %collective-permute-start.7 = (f32[2,512,128]{2,1,0:T(8,128)S(1)}, f32[2,512,128]{2,1,0:T(8,128)S(1)}, u32[]{:S(2)}, u32[]{:S(2)}) collective-permute-start(f32[2,512,128]{2,1,0:T(8,128)S(1)} %bitcast.212), channel_id=1, source_target_pairs={{0,24},{8,16},{32,56},{40,48},{64,88},{72,80},{96,120},{104,112},{... | collective-permute-start | bytes 1572872 | tf_op jit(solution)/shard_map/ppermute | solution.py:480
  55.1 3.4 %collective-permute-start.4 = (f32[528,128]{1,0:T(8,128)S(1)}, f32[528,128]{1,0:T(8,128)S(1)}, u32[]{:S(2)}, u32[]{:S(2)}) collective-permute-start(f32[528,128]{1,0:T(8,128)S(1)} %pad_maximum_fusion.1), channel_id=1, source_target_pairs={{0,64},{8,72},{16,80},{24,88},{32,96},{40,104},{48,112},{56,120},{... | collective-permute-start | bytes 811016 | tf_op jit(solution)/shard_map/ppermute | solution.py:480
  59.3 0.9 add_select_fusion
  60.1 9.4 %collective-permute-done.4.refs_6_.refs_17_ = f32[528,128]{1,0:T(8,128)S(1)} collective-permute-done((f32[528,128]{1,0:T(8,128)S(1)}, f32[528,128]{1,0:T(8,128)S(1)}, u32[]{:S(2)}, u32[]{:S(2)}) %collective-permute-start.4) | collective-permute-done | bytes 270368 | tf_op jit(solution)/shard_map/ppermute | solution.py:480
  69.6 0.8 fusion.42
  70.4 5.3 %collective-permute-start.15 = (f32[528,128]{1,0:T(8,128)S(1)}, f32[528,128]{1,0:T(8,128)S(1)}, u32[]{:S(2)}, u32[]{:S(2)}) collective-permute-start(f32[528,128]{1,0:T(8,128)S(1)} %pad_maximum_fusion.2), channel_id=1, source_target_pairs={{0,224},{8,232},{16,240},{24,248},{32,192},{40,200},{48,208},{56,2... | collective-permute-start | bytes 811016 | tf_op jit(solution)/shard_map/ppermute | solution.py:480
  76.3 2.0 collective-permute-start.11
  78.3 0.8 broadcast_multiply_fusion
  79.3 2.8 %collective-permute-start.14 = (f32[528,128]{1,0:T(8,128)S(1)}, f32[528,128]{1,0:T(8,128)}, u32[]{:S(2)}, u32[]{:S(2)}) collective-permute-start(f32[528,128]{1,0:T(8,128)S(1)} %collective-permute-done.4.refs_6_.refs_17_), channel_id=1, source_target_pairs={{0,24},{8,16},{16,8},{24,0},{32,56},{40,48},{48,40},{56,32},{64,88... | collective-permute-start | bytes 811016 | tf_op jit(solution)/shard_map/ppermute | solution.py:480
  82.0 4.9 %collective-permute-done.15.refs_10_.refs_21_ = f32[528,128]{1,0:T(8,128)S(1)} collective-permute-done((f32[528,128]{1,0:T(8,128)S(1)}, f32[528,128]{1,0:T(8,128)S(1)}, u32[]{:S(2)}, u32[]{:S(2)}) %collective-permute-start.15) | collective-permute-done | bytes 270368 | tf_op jit(solution)/shard_map/ppermute | solution.py:480
  86.9 4.5 %collective-permute-done.11.refs_10_.refs_15_ = f32[528,128]{1,0:T(8,128)S(1)} collective-permute-done((f32[528,128]{1,0:T(8,128)S(1)}, f32[528,128]{1,0:T(8,128)S(1)}, u32[]{:S(2)}, u32[]{:S(2)}) %collective-permute-start.11) | collective-permute-done | bytes 270368 | tf_op jit(solution)/shard_map/ppermute | solution.py:480
  91.5 2.7 %collective-permute-start.18 = (f32[528,128]{1,0:T(8,128)S(1)}, f32[528,128]{1,0:T(8,128)}, u32[]{:S(2)}, u32[]{:S(2)}) collective-permute-start(f32[528,128]{1,0:T(8,128)S(1)} %collective-permute-done.15.refs_10_.refs_21_), channel_id=1, source_target_pairs={{0,24},{8,16},{16,8},{24,0},{32,56},{40,48},{48,40},{56,32},{64,88... | collective-permute-start | bytes 811016 | tf_op jit(solution)/shard_map/ppermute | solution.py:480
  94.2 0.6 copy.16
  94.9 6.6 %shard_map.146 = (f32[16,128,384]{2,1,0:T(8,128)}, f32[16,128,128]{2,1,0:T(8,128)}) custom-call(s32[1]{0:T(128)} %bitcast.x_ref.refs_0_, bf16[128,2048]{1,0:T(8,128)(2,1)} %refs_1_.7, f32[16,128,128]{2,1,0:T(8,128)} %shard_map.145.refs_2_, f32[4,32,128]{2,1,0:T(8,128)} %bitcast.199, f32[2,512,128]{2,1,0:T(8,128)} %copy-done.1, f32[2,512,128]{2,1,0:T(8,128)} %copy-done, ...), custom_call_target="tpu_custom_call" | custom-call | tf_op jit(solution)/shard_map/pallas_call | solution.py:449
  101.6 1.6 collective-permute-done.16.refs_11_.refs_22_
  103.2 3.2 %collective-permute-done.17.refs_12_.refs_23_ = f32[528,128]{1,0:T(8,128)} collective-permute-done((f32[528,128]{1,0:T(8,128)S(1)}, f32[528,128]{1,0:T(8,128)}, u32[]{:S(2)}, u32[]{:S(2)}) %collective-permute-start.17) | collective-permute-done | bytes 270368 | tf_op jit(solution)/shard_map/ppermute | solution.py:480
  106.4 9.7 %shard_map.147 = (f32[16,128,256]{2,1,0:T(8,128)}, f32[16,128,128]{2,1,0:T(8,128)}, f32[520,128]{1,0:T(8,128)}, f32[520,128]{1,0:T(8,128)}, f32[520,128]{1,0:T(8...) custom-call(s32[1]{0:T(128)} %bitcast.x_ref.refs_0_, ...), custom_call_target="tpu_custom_call" | custom-call | tf_op jit(solution)/shard_map/pallas_call | solution.py:449
  116.5 1.7 collective-permute-start.23
  118.1 3.1 %collective-permute-start.24 = (f32[520,128]{1,0:T(8,128)}, f32[520,128]{1,0:T(8,128)S(1)}, u32[]{:S(2)}, u32[]{:S(2)}) collective-permute-start(f32[520,128]{1,0:T(8,128)} %get-tuple-element.65), channel_id=1, source_target_pairs={{0,16},{8,24},{16,0},{24,8},{32,48},{40,56},{48,32},{56,40},{64,80... | collective-permute-start | bytes 798728 | tf_op jit(solution)/shard_map/ppermute | solution.py:480
  121.7 1.0 slice.301
  122.8 8.2 %shard_map.149 = (f32[4,512,128]{2,1,0:T(8,128)}, f32[2,512,128]{2,1,0:T(8,128)}, f32[2,512,128]{2,1,0:T(8,128)}, f32[4,32,128]{2,1,0:T(8,128)}) custom-call(s32[1]{0:T(128)} %bitcast.x_ref.refs_0_, bf16[128,2048]{1,0:T(8,128)(2,1)} %refs_1_.7, f32[16,128,128]{2,1,0:T(8,128)} %shard_map.145.refs_2_, f32[4,32,128]{2,1,0:T(8,128)} %bitcast.201, ...), custom_call_target="tpu_custom_call" | custom-call | tf_op jit(solution)/shard_map/pallas_call | solution.py:449
  131.0 0.9 collective-permute-start.30
  131.9 4.9 %collective-permute-done.23 = f32[520,128]{1,0:T(8,128)S(1)} collective-permute-done((f32[520,128]{1,0:T(8,128)}, f32[520,128]{1,0:T(8,128)S(1)}, u32[]{:S(2)}, u32[]{:S(2)}) %collective-permute-start.23) | collective-permute-done | bytes 266272 | tf_op jit(solution)/shard_map/ppermute | solution.py:480
  136.8 1.3 collective-permute-start.19
  138.1 7.5 %collective-permute-done.24 = f32[520,128]{1,0:T(8,128)S(1)} collective-permute-done((f32[520,128]{1,0:T(8,128)}, f32[520,128]{1,0:T(8,128)S(1)}, u32[]{:S(2)}, u32[]{:S(2)}) %collective-permute-start.24) | collective-permute-done | bytes 266272 | tf_op jit(solution)/shard_map/ppermute | solution.py:480
  145.9 1.1 collective-permute-start.26
  147.0 2.1 collective-permute-start.28
  149.1 2.1 collective-permute-done.30
  151.2 3.7 %collective-permute-start.31 = (f32[512,128]{1,0:T(8,128)S(1)}, f32[512,128]{1,0:T(8,128)S(1)}, u32[]{:S(2)}, u32[]{:S(2)}) collective-permute-start(f32[512,128]{1,0:T(8,128)S(1)} %fusion.16), channel_id=1, source_target_pairs={{0,24},{8,16},{16,8},{24,0},{32,56},{40,48},{48,40},{56,32},{64,88... | collective-permute-start | bytes 786440 | tf_op jit(solution)/shard_map/ppermute | solution.py:480
  154.9 1.5 collective-permute-done.26
  156.4 5.0 %collective-permute-done.28 = f32[512,128]{1,0:T(8,128)S(1)} collective-permute-done((f32[512,128]{1,0:T(8,128)S(1)}, f32[512,128]{1,0:T(8,128)S(1)}, u32[]{:S(2)}, u32[]{:S(2)}) %collective-permute-start.28) | collective-permute-done | bytes 262176 | tf_op jit(solution)/shard_map/ppermute | solution.py:480
  161.7 0.7 collective-permute-start.29
  162.4 1.3 collective-permute-start.20
  163.8 1.9 collective-permute-start.22
  165.8 0.7 collective-permute-done.31
  166.5 4.9 %collective-permute-done.29 = f32[520,128]{1,0:T(8,128)S(1)} collective-permute-done((f32[520,128]{1,0:T(8,128)S(1)}, f32[520,128]{1,0:T(8,128)S(1)}, u32[]{:S(2)}, u32[]{:S(2)}) %collective-permute-start.29) | collective-permute-done | bytes 266272 | tf_op jit(solution)/shard_map/ppermute | solution.py:480
  171.6 0.7 pad_maximum_fusion.5
  172.4 3.3 %collective-permute-done.20.p1_ref = f32[2,512,128]{2,1,0:T(8,128)S(1)} collective-permute-done((f32[2,512,128]{2,1,0:T(8,128)S(1)}, f32[2,512,128]{2,1,0:T(8,128)S(1)}, u32[]{:S(2)}, u32[]{:S(2)}) %collective-permute-start.20) | collective-permute-done | bytes 524320 | tf_op jit(solution)/shard_map/ppermute | solution.py:480
  175.7 0.9 multiply_add_fusion.1
  176.6 2.1 collective-permute-start.21
  178.8 1.4 select_bitcast_fusion
  180.2 10.3 %shard_map.148 = (bf16[128,2048]{1,0:T(8,128)(2,1)}, f32[16,128,128]{2,1,0:T(8,128)}, f32[16,128,128]{2,1,0:T(8,128)}) custom-call(s32[1]{0:T(128)} %bitcast.x_ref.refs_0_, bf16[128,2048]{1,0:T(8,128)(2,1)} %refs_1_.7, bf16[128,2048]{1,0:T(8,128)(2,1)} %key_ref.5, f32[4,128,8]{2,1,0:T(8,128)} %get-tuple-element.41.cols_ref.refs_3_, ...), custom_call_target="tpu_custom_call" | custom-call | tf_op jit(solution)/shard_map/pallas_call | solution.py:449
  190.6 1.1 fusion.9.a0_ref
  191.7 2.1 collective-permute-start.33
  193.8 2.8 %collective-permute-start.35 = (f32[512,128]{1,0:T(8,128)S(1)}, f32[512,128]{1,0:T(8,128)S(1)}, u32[]{:S(2)}, u32[]{:S(2)}) collective-permute-start(f32[512,128]{1,0:T(8,128)S(1)} %fusion.9.a0_ref), channel_id=1, source_target_pairs={{0,24},{8,16},{16,8},{24,0},{32,56},{40,48},{48,40},{56,32},{64,88... | collective-permute-start | bytes 786440 | tf_op jit(solution)/shard_map/ppermute | solution.py:480
  197.2 1.2 fusion.39
  198.5 1.5 collective-permute-done.33.a1_ref
  200.0 2.4 %collective-permute-done.34.a2_ref = f32[512,128]{1,0:T(8,128)S(1)} collective-permute-done((f32[512,128]{1,0:T(8,128)S(1)}, f32[512,128]{1,0:T(8,128)S(1)}, u32[]{:S(2)}, u32[]{:S(2)}) %collective-permute-start.34) | collective-permute-done | bytes 262176 | tf_op jit(solution)/shard_map/ppermute | solution.py:480
  202.4 2.7 %collective-permute-done.35.a3_ref = f32[512,128]{1,0:T(8,128)S(1)} collective-permute-done((f32[512,128]{1,0:T(8,128)S(1)}, f32[512,128]{1,0:T(8,128)S(1)}, u32[]{:S(2)}, u32[]{:S(2)}) %collective-permute-start.35) | collective-permute-done | bytes 262176 | tf_op jit(solution)/shard_map/ppermute | solution.py:480
  205.2 0.7 copy-done.26
  205.8 8.9 %shard_map.150 = (bf16[128,2048]{1,0:T(8,128)(2,1)}, bf16[128,2048]{1,0:T(8,128)(2,1)}, f32[4,8,128]{2,1,0:T(8,128)}) custom-call(s32[1]{0:T(128)} %bitcast.x_ref.refs_0_, bf16[128,2048]{1,0:T(8,128)(2,1)} %key_ref.5, bf16[128,2048]{1,0:T(8,128)(2,1)} %value_ref.3, f32[4,128,8]{2,1,0:T(8,128)} %get-tuple-element.41.cols_ref.refs_3_, ...), custom_call_target="tpu_custom_call" | custom-call | tf_op jit(solution)/shard_map/pallas_call | solution.py:449
  214.8 1.3 slice.249
  (150 shorter events, 7.8 us)
Async XLA Ops:
  13.2 16.3 %copy-start.28 = (f32[4,8,128]{2,1,0:T(8,128)S(1)}, f32[4,8,128]{2,1,0:T(8,128)}, u32[]{:S(2)}) copy-start(f32[4,8,128]{2,1,0:T(8,128)} %get-tuple-element.42.rows_ref.refs_4_) | copy-start | bytes 49156
  13.3 19.2 %copy-start.31 = (f32[16,128]{1,0:T(8,128)S(1)}, f32[16,128]{1,0:T(8,128)}, u32[]{:S(2)}) copy-start(f32[16,128]{1,0:T(8,128)} %get-tuple-element.48) | copy-start | bytes 24580
  13.3 19.3 %copy-start.27 = (f32[528,128]{1,0:T(8,128)S(1)}, f32[528,128]{1,0:T(8,128)}, u32[]{:S(2)}) copy-start(f32[528,128]{1,0:T(8,128)} %get-tuple-element.47) | copy-start | bytes 811012
  13.3 16.2 %collective-permute-start = (f32[528,128]{1,0:T(8,128)}, f32[528,128]{1,0:T(8,128)S(1)}, u32[]{:S(2)}, u32[]{:S(2)}) collective-permute-start(f32[528,128]{1,0:T(8,128)} %get-tuple-element.44), channel_id=1, source_target_pairs={{0,8},{8,0},{16,24},{24,16},{32,40},{40,32},{48,56},{56,48},{64,72... | collective-permute-start | bytes 811016 | tf_op jit(solution)/shard_map/ppermute | solution.py:480
  14.9 16.1 %collective-permute-start.1 = (f32[528,128]{1,0:T(8,128)}, f32[528,128]{1,0:T(8,128)S(1)}, u32[]{:S(2)}, u32[]{:S(2)}) collective-permute-start(f32[528,128]{1,0:T(8,128)} %get-tuple-element.45), channel_id=1, source_target_pairs={{0,16},{8,24},{16,0},{24,8},{32,48},{40,56},{48,32},{56,40},{64,80... | collective-permute-start | bytes 811016 | tf_op jit(solution)/shard_map/ppermute | solution.py:480
  17.6 14.9 %collective-permute-start.2 = (f32[528,128]{1,0:T(8,128)}, f32[528,128]{1,0:T(8,128)S(1)}, u32[]{:S(2)}, u32[]{:S(2)}) collective-permute-start(f32[528,128]{1,0:T(8,128)} %get-tuple-element.46), channel_id=1, source_target_pairs={{0,24},{8,16},{16,8},{24,0},{32,56},{40,48},{48,40},{56,32},{64,88... | collective-permute-start | bytes 811016 | tf_op jit(solution)/shard_map/ppermute | solution.py:480
  18.1 21.9 %collective-permute-start.6 = (f32[2,512,128]{2,1,0:T(8,128)}, f32[2,512,128]{2,1,0:T(8,128)S(1)}, u32[]{:S(2)}, u32[]{:S(2)}) collective-permute-start(f32[2,512,128]{2,1,0:T(8,128)} %get-tuple-element.51), channel_id=1, source_target_pairs={{0,8},{8,0},{16,24},{32,40},{40,32},{48,56},{64,72},{72,64},{80,88... | collective-permute-start | bytes 1572872 | tf_op jit(solution)/shard_map/ppermute | solution.py:480
  20.3 29.9 %collective-permute-start.5 = (f32[2,512,128]{2,1,0:T(8,128)}, f32[2,512,128]{2,1,0:T(8,128)S(1)}, u32[]{:S(2)}, u32[]{:S(2)}) collective-permute-start(f32[2,512,128]{2,1,0:T(8,128)} %get-tuple-element.50), channel_id=1, source_target_pairs={{0,8},{8,0},{16,24},{32,40},{40,32},{48,56},{64,72},{72,64},{80,88... | collective-permute-start | bytes 1572872 | tf_op jit(solution)/shard_map/ppermute | solution.py:480
  24.7 146.7 %copy-start.32 = (pred[512]{0:T(512)(128)(4,1)}, pred[512]{0:T(512)(128)(4,1)S(1)}, u32[]{:S(2)}) copy-start(pred[512]{0:T(512)(128)(4,1)S(1)} %broadcast_in_dim.82) | copy-start | bytes 1540
  24.7 15.3 %copy-start.17 = (f32[2,512,128]{2,1,0:T(8,128)S(1)}, f32[2,512,128]{2,1,0:T(8,128)}, u32[]{:S(2)}) copy-start(f32[2,512,128]{2,1,0:T(8,128)} %get-tuple-element.51) | copy-start | bytes 1572868
  29.5 20.6 %copy-start.16 = (f32[2,512,128]{2,1,0:T(8,128)S(1)}, f32[2,512,128]{2,1,0:T(8,128)}, u32[]{:S(2)}) copy-start(f32[2,512,128]{2,1,0:T(8,128)} %get-tuple-element.50) | copy-start | bytes 1572868
  32.7 22.2 %collective-permute-start.3 = (f32[528,128]{1,0:T(8,128)S(1)}, f32[528,128]{1,0:T(8,128)S(1)}, u32[]{:S(2)}, u32[]{:S(2)}) collective-permute-start(f32[528,128]{1,0:T(8,128)S(1)} %pad_maximum_fusion), channel_id=1, source_target_pairs={{0,32},{8,40},{16,48},{24,56},{32,0},{40,8},{48,16},{56,24},{64,96... | collective-permute-start | bytes 811016 | tf_op jit(solution)/shard_map/ppermute | solution.py:480
  40.0 20.1 %copy-start = (f32[2,512,128]{2,1,0:T(8,128)}, f32[2,512,128]{2,1,0:T(8,128)S(1)}, u32[]{:S(2)}) copy-start(f32[2,512,128]{2,1,0:T(8,128)S(1)} %collective-permute-done.6.refs_5_.refs_10_) | copy-start | bytes 1572868
  40.1 39.0 %collective-permute-start.8 = (f32[2,512,128]{2,1,0:T(8,128)S(1)}, f32[2,512,128]{2,1,0:T(8,128)S(1)}, u32[]{:S(2)}, u32[]{:S(2)}) collective-permute-start(f32[2,512,128]{2,1,0:T(8,128)S(1)} %bitcast.211), channel_id=1, source_target_pairs={{0,24},{8,16},{32,56},{40,48},{64,88},{72,80},{96,120},{104,112},{... | collective-permute-start | bytes 1572872 | tf_op jit(solution)/shard_map/ppermute | solution.py:480
  50.1 20.3 %copy-start.1 = (f32[2,512,128]{2,1,0:T(8,128)}, f32[2,512,128]{2,1,0:T(8,128)S(1)}, u32[]{:S(2)}) copy-start(f32[2,512,128]{2,1,0:T(8,128)S(1)} %collective-permute-done.5.refs_4_.refs_9_) | copy-start | bytes 1572868
  50.1 29.0 %copy-start.29 = (f32[128,16,6]{0,1,2:T(8,128)S(1)}, f32[128,16,6]{0,1,2:T(8,128)}, u32[]{:S(2)}) copy-start(f32[128,16,6]{0,1,2:T(8,128)} %param.14) | copy-start | bytes 147460
  50.2 29.1 %collective-permute-start.7 = (f32[2,512,128]{2,1,0:T(8,128)S(1)}, f32[2,512,128]{2,1,0:T(8,128)S(1)}, u32[]{:S(2)}, u32[]{:S(2)}) collective-permute-start(f32[2,512,128]{2,1,0:T(8,128)S(1)} %bitcast.212), channel_id=1, source_target_pairs={{0,24},{8,16},{32,56},{40,48},{64,88},{72,80},{96,120},{104,112},{... | collective-permute-start | bytes 1572872 | tf_op jit(solution)/shard_map/ppermute | solution.py:480
  54.9 39.9 %copy-start.2 = (f32[528,128]{1,0:T(8,128)}, f32[528,128]{1,0:T(8,128)S(1)}, u32[]{:S(2)}) copy-start(f32[528,128]{1,0:T(8,128)S(1)} %collective-permute-done.3.refs_8_.refs_13_) | copy-start | bytes 811012
  55.1 14.5 %collective-permute-start.4 = (f32[528,128]{1,0:T(8,128)S(1)}, f32[528,128]{1,0:T(8,128)S(1)}, u32[]{:S(2)}, u32[]{:S(2)}) collective-permute-start(f32[528,128]{1,0:T(8,128)S(1)} %pad_maximum_fusion.1), channel_id=1, source_target_pairs={{0,64},{8,72},{16,80},{24,88},{32,96},{40,104},{48,112},{56,120},{... | collective-permute-start | bytes 811016 | tf_op jit(solution)/shard_map/ppermute | solution.py:480
  58.5 17.9 %collective-permute-start.10 = (f32[528,128]{1,0:T(8,128)S(1)}, f32[528,128]{1,0:T(8,128)S(1)}, u32[]{:S(2)}, u32[]{:S(2)}) collective-permute-start(f32[528,128]{1,0:T(8,128)S(1)} %collective-permute-done.3.refs_8_.refs_13_), channel_id=1, source_target_pairs={{0,24},{8,16},{16,8},{24,0},{32,56},{40,48},{48,40},{56,32},{64,88... | collective-permute-start | bytes 811016 | tf_op jit(solution)/shard_map/ppermute | solution.py:480
  58.6 17.8 %collective-permute-start.9 = (f32[528,128]{1,0:T(8,128)S(1)}, f32[528,128]{1,0:T(8,128)S(1)}, u32[]{:S(2)}, u32[]{:S(2)}) collective-permute-start(f32[528,128]{1,0:T(8,128)S(1)} %collective-permute-done.3.refs_8_.refs_13_), channel_id=1, source_target_pairs={{0,8},{8,0},{16,24},{24,16},{32,40},{40,32},{48,56},{56,48},{64,72... | collective-permute-start | bytes 811016 | tf_op jit(solution)/shard_map/ppermute | solution.py:480
  69.6 32.0 %copy-start.3 = (f32[528,128]{1,0:T(8,128)}, f32[528,128]{1,0:T(8,128)S(1)}, u32[]{:S(2)}) copy-start(f32[528,128]{1,0:T(8,128)S(1)} %collective-permute-done.4.refs_6_.refs_17_) | copy-start | bytes 811012
  70.4 16.6 %collective-permute-start.15 = (f32[528,128]{1,0:T(8,128)S(1)}, f32[528,128]{1,0:T(8,128)S(1)}, u32[]{:S(2)}, u32[]{:S(2)}) collective-permute-start(f32[528,128]{1,0:T(8,128)S(1)} %pad_maximum_fusion.2), channel_id=1, source_target_pairs={{0,224},{8,232},{16,240},{24,248},{32,192},{40,200},{48,208},{56,2... | collective-permute-start | bytes 811016 | tf_op jit(solution)/shard_map/ppermute | solution.py:480
  76.3 18.5 %copy-start.9 = (f32[528,128]{1,0:T(8,128)}, f32[528,128]{1,0:T(8,128)S(1)}, u32[]{:S(2)}) copy-start(f32[528,128]{1,0:T(8,128)S(1)} %collective-permute-done.10.refs_11_.refs_16_) | copy-start | bytes 811012
  76.3 15.2 %collective-permute-start.12 = (f32[528,128]{1,0:T(8,128)S(1)}, f32[528,128]{1,0:T(8,128)S(1)}, u32[]{:S(2)}, u32[]{:S(2)}) collective-permute-start(f32[528,128]{1,0:T(8,128)S(1)} %collective-permute-done.4.refs_6_.refs_17_), channel_id=1, source_target_pairs={{0,8},{8,0},{16,24},{24,16},{32,40},{40,32},{48,56},{56,48},{64,72... | collective-permute-start | bytes 811016 | tf_op jit(solution)/shard_map/ppermute | solution.py:480
  76.3 18.5 %copy-start.10 = (f32[528,128]{1,0:T(8,128)}, f32[528,128]{1,0:T(8,128)S(1)}, u32[]{:S(2)}) copy-start(f32[528,128]{1,0:T(8,128)S(1)} %collective-permute-done.9.refs_9_.refs_14_) | copy-start | bytes 811012
  76.3 15.1 %collective-permute-start.11 = (f32[528,128]{1,0:T(8,128)S(1)}, f32[528,128]{1,0:T(8,128)S(1)}, u32[]{:S(2)}, u32[]{:S(2)}) collective-permute-start(f32[528,128]{1,0:T(8,128)S(1)} %collective-permute-done.10.refs_11_.refs_16_), channel_id=1, source_target_pairs={{0,8},{8,0},{16,24},{24,16},{32,40},{40,32},{48,56},{56,48},{64,72... | collective-permute-start | bytes 811016 | tf_op jit(solution)/shard_map/ppermute | solution.py:480
  79.2 15.7 %copy-start.7 = (f32[2,512,128]{2,1,0:T(8,128)}, f32[2,512,128]{2,1,0:T(8,128)S(1)}, u32[]{:S(2)}) copy-start(f32[2,512,128]{2,1,0:T(8,128)S(1)} %collective-permute-done.8.refs_7_.refs_12_) | copy-start | bytes 1572868
  79.2 22.4 %collective-permute-start.13 = (f32[528,128]{1,0:T(8,128)S(1)}, f32[528,128]{1,0:T(8,128)S(1)}, u32[]{:S(2)}, u32[]{:S(2)}) collective-permute-start(f32[528,128]{1,0:T(8,128)S(1)} %collective-permute-done.4.refs_6_.refs_17_), channel_id=1, source_target_pairs={{0,16},{8,24},{16,0},{24,8},{32,48},{40,56},{48,32},{56,40},{64,80... | collective-permute-start | bytes 811016 | tf_op jit(solution)/shard_map/ppermute | solution.py:480
  79.3 15.6 %copy-start.8 = (f32[2,512,128]{2,1,0:T(8,128)}, f32[2,512,128]{2,1,0:T(8,128)S(1)}, u32[]{:S(2)}) copy-start(f32[2,512,128]{2,1,0:T(8,128)S(1)} %collective-permute-done.7.refs_6_.refs_11_) | copy-start | bytes 1572868
  79.3 22.3 %collective-permute-start.14 = (f32[528,128]{1,0:T(8,128)S(1)}, f32[528,128]{1,0:T(8,128)}, u32[]{:S(2)}, u32[]{:S(2)}) collective-permute-start(f32[528,128]{1,0:T(8,128)S(1)} %collective-permute-done.4.refs_6_.refs_17_), channel_id=1, source_target_pairs={{0,24},{8,16},{16,8},{24,0},{32,56},{40,48},{48,40},{56,32},{64,88... | collective-permute-start | bytes 811016 | tf_op jit(solution)/shard_map/ppermute | solution.py:480
  86.9 19.4 %copy-start.4 = (f32[528,128]{1,0:T(8,128)}, f32[528,128]{1,0:T(8,128)S(1)}, u32[]{:S(2)}) copy-start(f32[528,128]{1,0:T(8,128)S(1)} %collective-permute-done.15.refs_10_.refs_21_) | copy-start | bytes 811012
  86.9 16.2 %collective-permute-start.16 = (f32[528,128]{1,0:T(8,128)S(1)}, f32[528,128]{1,0:T(8,128)}, u32[]{:S(2)}, u32[]{:S(2)}) collective-permute-start(f32[528,128]{1,0:T(8,128)S(1)} %collective-permute-done.15.refs_10_.refs_21_), channel_id=1, source_target_pairs={{0,8},{8,0},{16,24},{24,16},{32,40},{40,32},{48,56},{56,48},{64,72... | collective-permute-start | bytes 811016 | tf_op jit(solution)/shard_map/ppermute | solution.py:480
  91.5 14.9 %collective-permute-start.17 = (f32[528,128]{1,0:T(8,128)S(1)}, f32[528,128]{1,0:T(8,128)}, u32[]{:S(2)}, u32[]{:S(2)}) collective-permute-start(f32[528,128]{1,0:T(8,128)S(1)} %collective-permute-done.15.refs_10_.refs_21_), channel_id=1, source_target_pairs={{0,16},{8,24},{16,0},{24,8},{32,48},{40,56},{48,32},{56,40},{64,80... | collective-permute-start | bytes 811016 | tf_op jit(solution)/shard_map/ppermute | solution.py:480
  91.5 14.9 %copy-start.11 = (f32[528,128]{1,0:T(8,128)}, f32[528,128]{1,0:T(8,128)S(1)}, u32[]{:S(2)}) copy-start(f32[528,128]{1,0:T(8,128)S(1)} %collective-permute-done.12.refs_7_.refs_18_) | copy-start | bytes 811012
  91.5 14.9 %collective-permute-start.18 = (f32[528,128]{1,0:T(8,128)S(1)}, f32[528,128]{1,0:T(8,128)}, u32[]{:S(2)}, u32[]{:S(2)}) collective-permute-start(f32[528,128]{1,0:T(8,128)S(1)} %collective-permute-done.15.refs_10_.refs_21_), channel_id=1, source_target_pairs={{0,24},{8,16},{16,8},{24,0},{32,56},{40,48},{48,40},{56,32},{64,88... | collective-permute-start | bytes 811016 | tf_op jit(solution)/shard_map/ppermute | solution.py:480
  116.0 31.0 %collective-permute-start.27 = (f32[2,512,128]{2,1,0:T(8,128)}, f32[2,512,128]{2,1,0:T(8,128)S(1)}, u32[]{:S(2)}, u32[]{:S(2)}) collective-permute-start(f32[2,512,128]{2,1,0:T(8,128)} %get-tuple-element.68), channel_id=1, source_target_pairs={{0,8},{8,0},{16,24},{24,16},{32,40},{40,32},{48,56},{56,48},{64,72... | collective-permute-start | bytes 1572872 | tf_op jit(solution)/shard_map/ppermute | solution.py:480
  116.5 20.4 %collective-permute-start.23 = (f32[520,128]{1,0:T(8,128)}, f32[520,128]{1,0:T(8,128)S(1)}, u32[]{:S(2)}, u32[]{:S(2)}) collective-permute-start(f32[520,128]{1,0:T(8,128)} %get-tuple-element.64), channel_id=1, source_target_pairs={{0,8},{8,0},{16,24},{24,16},{32,40},{40,32},{48,56},{56,48},{64,72... | collective-permute-start | bytes 798728 | tf_op jit(solution)/shard_map/ppermute | solution.py:480
  118.1 27.4 %collective-permute-start.24 = (f32[520,128]{1,0:T(8,128)}, f32[520,128]{1,0:T(8,128)S(1)}, u32[]{:S(2)}, u32[]{:S(2)}) collective-permute-start(f32[520,128]{1,0:T(8,128)} %get-tuple-element.65), channel_id=1, source_target_pairs={{0,16},{8,24},{16,0},{24,8},{32,48},{40,56},{48,32},{56,40},{64,80... | collective-permute-start | bytes 798728 | tf_op jit(solution)/shard_map/ppermute | solution.py:480
  121.3 24.3 %collective-permute-start.25 = (f32[520,128]{1,0:T(8,128)}, f32[520,128]{1,0:T(8,128)S(1)}, u32[]{:S(2)}, u32[]{:S(2)}) collective-permute-start(f32[520,128]{1,0:T(8,128)} %get-tuple-element.66), channel_id=1, source_target_pairs={{0,24},{8,16},{16,8},{24,0},{32,56},{40,48},{48,40},{56,32},{64,88... | collective-permute-start | bytes 798728 | tf_op jit(solution)/shard_map/ppermute | solution.py:480
  122.7 22.8 %copy-start.23 = (f32[520,128]{1,0:T(8,128)S(1)}, f32[520,128]{1,0:T(8,128)}, u32[]{:S(2)}) copy-start(f32[520,128]{1,0:T(8,128)} %get-tuple-element.63) | copy-start | bytes 798724
  122.7 22.9 %copy-start.21 = (f32[64,128]{1,0:T(8,128)S(1)}, f32[64,128]{1,0:T(8,128)}, u32[]{:S(2)}) copy-start(f32[64,128]{1,0:T(8,128)} %param.17) | copy-start | bytes 98308
  122.8 24.2 %copy-start.22 = (f32[2,512,128]{2,1,0:T(8,128)S(1)}, f32[2,512,128]{2,1,0:T(8,128)}, u32[]{:S(2)}) copy-start(f32[2,512,128]{2,1,0:T(8,128)} %get-tuple-element.67) | copy-start | bytes 1572868
  131.0 20.2 %copy-start.19 = (f32[2,512,128]{2,1,0:T(8,128)S(1)}, f32[2,512,128]{2,1,0:T(8,128)}, u32[]{:S(2)}) copy-start(f32[2,512,128]{2,1,0:T(8,128)} %get-tuple-element.69) | copy-start | bytes 1572868
  131.0 31.4 %copy-start.14 = (f32[4,512,128]{2,1,0:T(8,128)S(1)}, f32[4,512,128]{2,1,0:T(8,128)}, u32[]{:S(2)}) copy-start(f32[4,512,128]{2,1,0:T(8,128)} %get-tuple-element.62) | copy-start | bytes 3145732
  131.0 20.2 %collective-permute-start.30 = (f32[2,512,128]{2,1,0:T(8,128)}, f32[2,512,128]{2,1,0:T(8,128)S(1)}, u32[]{:S(2)}, u32[]{:S(2)}) collective-permute-start(f32[2,512,128]{2,1,0:T(8,128)} %get-tuple-element.70), channel_id=1, source_target_pairs={{0,8},{8,0},{16,24},{24,16},{32,40},{40,32},{48,56},{56,48},{64,72... | collective-permute-start | bytes 1572872 | tf_op jit(solution)/shard_map/ppermute | solution.py:480
  136.8 26.9 %collective-permute-start.19 = (f32[2,512,128]{2,1,0:T(8,128)}, f32[2,512,128]{2,1,0:T(8,128)S(1)}, u32[]{:S(2)}, u32[]{:S(2)}) collective-permute-start(f32[2,512,128]{2,1,0:T(8,128)} %get-tuple-element.58), channel_id=1, source_target_pairs={{16,8},{24,0},{48,40},{56,32},{80,72},{88,64},{112,104},{120,96},{... | collective-permute-start | bytes 1572872 | tf_op jit(solution)/shard_map/ppermute | solution.py:480
  145.8 16.6 %copy-start.34 = (f32[2,512,128]{2,1,0:T(8,128)S(1)}, f32[2,512,128]{2,1,0:T(8,128)}, u32[]{:S(2)}) copy-start(f32[2,512,128]{2,1,0:T(8,128)} %get-tuple-element.59) | copy-start | bytes 1572868
  145.9 10.6 %collective-permute-start.26 = (f32[520,128]{1,0:T(8,128)S(1)}, f32[520,128]{1,0:T(8,128)S(1)}, u32[]{:S(2)}, u32[]{:S(2)}) collective-permute-start(f32[520,128]{1,0:T(8,128)S(1)} %pad_maximum_fusion.3), channel_id=1, source_target_pairs={{0,224},{8,232},{16,240},{24,248},{32,192},{40,200},{48,208},{56,2... | collective-permute-start | bytes 798728 | tf_op jit(solution)/shard_map/ppermute | solution.py:480
  147.0 14.4 %collective-permute-start.28 = (f32[512,128]{1,0:T(8,128)S(1)}, f32[512,128]{1,0:T(8,128)S(1)}, u32[]{:S(2)}, u32[]{:S(2)}) collective-permute-start(f32[512,128]{1,0:T(8,128)S(1)} %fusion.19), channel_id=1, source_target_pairs={{0,24},{8,16},{16,8},{24,0},{32,56},{40,48},{48,40},{56,32},{64,88... | collective-permute-start | bytes 786440 | tf_op jit(solution)/shard_map/ppermute | solution.py:480
  151.2 15.2 %collective-permute-start.31 = (f32[512,128]{1,0:T(8,128)S(1)}, f32[512,128]{1,0:T(8,128)S(1)}, u32[]{:S(2)}, u32[]{:S(2)}) collective-permute-start(f32[512,128]{1,0:T(8,128)S(1)} %fusion.16), channel_id=1, source_target_pairs={{0,24},{8,16},{16,8},{24,0},{32,56},{40,48},{48,40},{56,32},{64,88... | collective-permute-start | bytes 786440 | tf_op jit(solution)/shard_map/ppermute | solution.py:480
  161.7 9.8 %collective-permute-start.29 = (f32[520,128]{1,0:T(8,128)S(1)}, f32[520,128]{1,0:T(8,128)S(1)}, u32[]{:S(2)}, u32[]{:S(2)}) collective-permute-start(f32[520,128]{1,0:T(8,128)S(1)} %pad_maximum_fusion.4), channel_id=1, source_target_pairs={{0,64},{8,72},{16,80},{24,88},{32,96},{40,104},{48,112},{56,120},{... | collective-permute-start | bytes 798728 | tf_op jit(solution)/shard_map/ppermute | solution.py:480
  162.4 17.8 %copy-start.30 = (f32[4,32,128]{2,1,0:T(8,128)S(1)}, f32[4,32,128]{2,1,0:T(8,128)}, u32[]{:S(2)}) copy-start(f32[4,32,128]{2,1,0:T(8,128)} %get-tuple-element.74) | copy-start | bytes 196612
  162.4 13.2 %collective-permute-start.20 = (f32[2,512,128]{2,1,0:T(8,128)S(1)}, f32[2,512,128]{2,1,0:T(8,128)S(1)}, u32[]{:S(2)}, u32[]{:S(2)}) collective-permute-start(f32[2,512,128]{2,1,0:T(8,128)S(1)} %copy-done.34), channel_id=1, source_target_pairs={{16,8},{24,0},{48,40},{56,32},{80,72},{88,64},{112,104},{120,96},{... | collective-permute-start | bytes 1572872 | tf_op jit(solution)/shard_map/ppermute | solution.py:480
  163.7 26.8 %copy-start.5 = (f32[2,512,128]{2,1,0:T(8,128)}, f32[2,512,128]{2,1,0:T(8,128)S(1)}, u32[]{:S(2)}) copy-start(f32[2,512,128]{2,1,0:T(8,128)S(1)} %collective-permute-done.19.p0_ref) | copy-start | bytes 1572868
  163.8 34.6 %collective-permute-start.22 = (f32[2,512,128]{2,1,0:T(8,128)S(1)}, f32[2,512,128]{2,1,0:T(8,128)S(1)}, u32[]{:S(2)}, u32[]{:S(2)}) collective-permute-start(f32[2,512,128]{2,1,0:T(8,128)S(1)} %bitcast.210), channel_id=1, source_target_pairs={{0,8},{8,0},{24,16},{32,40},{40,32},{56,48},{64,72},{72,64},{88,80... | collective-permute-start | bytes 1572872 | tf_op jit(solution)/shard_map/ppermute | solution.py:480
  172.4 18.2 %collective-permute-start.32 = (f32[520,128]{1,0:T(8,128)}, f32[520,128]{1,0:T(8,128)}, u32[]{:S(2)}, u32[]{:S(2)}) collective-permute-start(f32[520,128]{1,0:T(8,128)} %pad_maximum_fusion.5), channel_id=1, source_target_pairs={{0,32},{8,40},{16,48},{24,56},{32,0},{40,8},{48,16},{56,24},{64,96... | collective-permute-start | bytes 798728 | tf_op jit(solution)/shard_map/ppermute | solution.py:480
  175.7 14.9 %copy-start.6 = (f32[2,512,128]{2,1,0:T(8,128)}, f32[2,512,128]{2,1,0:T(8,128)S(1)}, u32[]{:S(2)}) copy-start(f32[2,512,128]{2,1,0:T(8,128)S(1)} %collective-permute-done.20.p1_ref) | copy-start | bytes 1572868
  176.6 21.8 %collective-permute-start.21 = (f32[2,512,128]{2,1,0:T(8,128)}, f32[2,512,128]{2,1,0:T(8,128)S(1)}, u32[]{:S(2)}, u32[]{:S(2)}) collective-permute-start(f32[2,512,128]{2,1,0:T(8,128)} %bitcast.57), channel_id=1, source_target_pairs={{0,8},{8,0},{24,16},{32,40},{40,32},{56,48},{64,72},{72,64},{88,80... | collective-permute-start | bytes 1572872 | tf_op jit(solution)/shard_map/ppermute | solution.py:480
  180.2 10.4 %copy-start.33 = (pred[512]{0:T(512)(128)(4,1)S(1)}, pred[512]{0:T(512)(128)(4,1)}, u32[]{:S(2)}) copy-start(pred[512]{0:T(512)(128)(4,1)} %copy-done.32) | copy-start | bytes 1540
  191.7 13.4 %copy-start.15 = (f32[512,128]{1,0:T(8,128)}, f32[512,128]{1,0:T(8,128)S(1)}, u32[]{:S(2)}) copy-start(f32[512,128]{1,0:T(8,128)S(1)} %fusion.9.a0_ref) | copy-start | bytes 786436
  191.7 8.2 %collective-permute-start.33 = (f32[512,128]{1,0:T(8,128)S(1)}, f32[512,128]{1,0:T(8,128)S(1)}, u32[]{:S(2)}, u32[]{:S(2)}) collective-permute-start(f32[512,128]{1,0:T(8,128)S(1)} %fusion.9.a0_ref), channel_id=1, source_target_pairs={{0,8},{8,0},{16,24},{24,16},{32,40},{40,32},{48,56},{56,48},{64,72... | collective-permute-start | bytes 786440 | tf_op jit(solution)/shard_map/ppermute | solution.py:480
  193.8 8.6 %collective-permute-start.34 = (f32[512,128]{1,0:T(8,128)S(1)}, f32[512,128]{1,0:T(8,128)S(1)}, u32[]{:S(2)}, u32[]{:S(2)}) collective-permute-start(f32[512,128]{1,0:T(8,128)S(1)} %fusion.9.a0_ref), channel_id=1, source_target_pairs={{0,16},{8,24},{16,0},{24,8},{32,48},{40,56},{48,32},{56,40},{64,80... | collective-permute-start | bytes 786440 | tf_op jit(solution)/shard_map/ppermute | solution.py:480
  193.8 11.3 %collective-permute-start.35 = (f32[512,128]{1,0:T(8,128)S(1)}, f32[512,128]{1,0:T(8,128)S(1)}, u32[]{:S(2)}, u32[]{:S(2)}) collective-permute-start(f32[512,128]{1,0:T(8,128)S(1)} %fusion.9.a0_ref), channel_id=1, source_target_pairs={{0,24},{8,16},{16,8},{24,0},{32,56},{40,48},{48,40},{56,32},{64,88... | collective-permute-start | bytes 786440 | tf_op jit(solution)/shard_map/ppermute | solution.py:480
  (7 other events, 30.3 us)
